TPU v7x, 256 devices: a whole 4x4x8 slice. The times are simulated.
256 devices in a mesh: tiles: 128 (over z, y_hi, x, core), cls: 2 (over y_lo).
Axes of the slice: x: 4, y: 4 (y_hi: 2, y_lo: 2; y = y_hi * 2 + y_lo), z: 8, core: 2. Of those that a mesh axis runs over, the one named last changes fastest.
Arguments:
- scaling: float32 [4, 2048, 8192], P('cls', 'tiles'), may hold values from 0.5 to 2
- source: float32 [4, 2048, 8192], P('cls', 'tiles'), may hold values from 0.3 to 4.5
- speed: float32 [4, 2048, 8192], P('cls', 'tiles'), may hold values from 0.3 to 1.5
- tile_mask: int32 [8, 32], replicated, may hold values from 0 to 1, as said below
- target: float32 [4], P('cls'), may hold values from 0.5 to 2
Outputs:
- heat_field: float32 [4, 2048, 8192], P('cls', 'tiles')
- flow_scaling: float32 [4, 2048, 8192], P('cls', 'tiles')
Inputs may be any that keep to these rules, and one draw needn't show every extreme that they name: `tile_mask`: 1 marks a land tile, 0 a sea tile; every row of tiles holds at least one land tile.
All inputs are finite; a program needn't handle non-finite values.
Results may differ from a plain program's by a relative error of at most 0.0001.
Values sent between devices are 32-bit elements; how exact they have to be, the bound alone decides.
A program may use at most 128 MiB of HBM per device.

v0:
```python
import jax
import jax.numpy as jnp
from jax import lax
from jax.sharding import PartitionSpec as P

TS = 256
NU = 2
J1 = 8


OMEGA_DAMP = 0.8
FINE_STRENGTH = 8.0
COARSE_SCALE = 16.0
COARSE_STRENGTH = 32.0
FLOOR_LEVEL = 0.25
directions = (
    (-1, 0, 1.0),
    (1, 0, 1.0),
    (0, -1, 1.0),
    (0, 1, 1.0),
    (-1, -1, 0.5),
    (-1, 1, 0.5),
    (1, -1, 0.5),
    (1, 1, 0.5),
)


def with_halo(array, sides, width):
    for axis, dim in sides:
        devices, length = (lax.axis_size(axis), array.shape[dim])
        up = [(i, (i + 1) % devices) for i in range(devices - 1)]
        down = [(j, i) for i, j in up]
        last = lax.slice_in_dim(array, length - width, length, axis=dim)
        leading = lax.slice_in_dim(array, 0, width, axis=dim)
        before = lax.ppermute(last, axis, up)
        after = lax.ppermute(leading, axis, down)
        array = jnp.concatenate([before, array, after], axis=dim)
    return array


def coefficients(speed_wide, diag_scale, strength):
    row_count = speed_wide.shape[1] - 2
    col_count = speed_wide.shape[2]
    speed_pad = jnp.pad(speed_wide, ((0, 0), (0, 0), (1, 1)))
    near_speed = jnp.zeros((speed_wide.shape[0], row_count, col_count), jnp.float32)
    for row_step, col_step, weight in directions:
        near_speed = (
            near_speed
            + weight
            * speed_pad[
                :, 1 + row_step : 1 + row_step + row_count, 1 + col_step : 1 + col_step + col_count
            ]
        )
    coupling = strength * speed_wide[:, 1 : row_count + 1, :]
    diagonal = diag_scale + coupling * near_speed
    return (speed_pad, coupling, diagonal)


def operate(field_wide, coeffs):
    speed_pad, coupling, diagonal = coeffs
    row_count = field_wide.shape[1] - 2
    col_count = field_wide.shape[2]
    padded = jnp.pad(field_wide, ((0, 0), (0, 0), (1, 1)))
    near_field = jnp.zeros_like(diagonal)
    for row_step, col_step, weight in directions:
        other_speed = speed_pad[
            :, 1 + row_step : 1 + row_step + row_count, 1 + col_step : 1 + col_step + col_count
        ]
        other_field = padded[
            :, 1 + row_step : 1 + row_step + row_count, 1 + col_step : 1 + col_step + col_count
        ]
        near_field = near_field + weight * other_speed * other_field
    center = field_wide[:, 1 : row_count + 1, :]
    return (diagonal * center - coupling * near_field, center)


def jacobi(field_wide, right_side, land_cells, coeffs):
    applied, center = operate(field_wide, coeffs)
    return land_cells * (center + OMEGA_DAMP * (right_side - applied) / coeffs[2])


def land_band(tile_mask, first_row, row_total, stride):
    tile_count = tile_mask.shape[0]
    global_rows = first_row + stride * jnp.arange(row_total, dtype=jnp.int32)
    tile_rows = global_rows // TS
    picker = (tile_rows[:, None] == jnp.arange(tile_count, dtype=jnp.int32)[None, :]).astype(
        jnp.float32
    )
    land_rows = jnp.dot(picker, tile_mask.astype(jnp.float32), precision=lax.Precision.HIGHEST)
    return jnp.repeat(land_rows, TS // stride, axis=1)[None]


def block_mean(field):
    shaped = field.reshape(field.shape[0], field.shape[1] // 4, 4, field.shape[2] // 4, 4)
    return jnp.mean(shaped, axis=(2, 4))


def block_sum(field):
    shaped = field.reshape(field.shape[0], field.shape[1] // 4, 4, field.shape[2] // 4, 4)
    return jnp.sum(shaped, axis=(2, 4))


def upsample(field):
    return jnp.repeat(jnp.repeat(field, 4, axis=1), 4, axis=2)


def fine_rim(field):
    return with_halo(field, (("tiles", 1),), 1)


def coarse_rim(field):
    return with_halo(field, (("tiles", 1),), 1)


def on_device(scaling, source, speed, tile_mask, target):
    class_count, row_count, col_count = scaling.shape
    quarter = row_count // 4
    row_start = lax.axis_index("tiles") * row_count
    land_cells = land_band(tile_mask, row_start, row_count, 1)
    coarse_land = land_band(tile_mask, row_start, quarter, 4)
    coarse_shape = (class_count, quarter, col_count // 4)
    global_mass = lax.psum(jnp.sum(source), ("tiles", "cls"))
    cell_total = float(scaling.size * lax.axis_size("tiles") * lax.axis_size("cls"))
    coarse_speed = block_mean(speed)
    speed_wide = with_halo(speed, (("tiles", 1),), 1)
    fine_coeffs = coefficients(speed_wide, 1.0, FINE_STRENGTH)

    def fine_sweeps(field):
        for sweep_index in range(NU):
            field = jacobi(fine_rim(field), scaling, land_cells, fine_coeffs)
        return field

    coarse_wide = with_halo(coarse_speed, (("tiles", 1),), 1)
    coarse_coeffs = coefficients(coarse_wide, COARSE_SCALE, COARSE_STRENGTH)
    field = jnp.zeros_like(scaling)
    pre_field = field
    pre_field = fine_sweeps(pre_field)
    applied, center = operate(fine_rim(pre_field), fine_coeffs)
    field = pre_field
    residual = land_cells * (scaling - applied)
    coarse_right = block_sum(residual)
    correction = jnp.zeros(coarse_shape, jnp.float32)
    for sweep_index in range(J1):
        correction = jacobi(coarse_rim(correction), coarse_right, coarse_land, coarse_coeffs)
    field = field + land_cells * upsample(correction)
    field = fine_sweeps(field)
    mass_ratio = target * cell_total / global_mass
    flow_scaling = land_cells * source * mass_ratio[:, None, None] / jnp.maximum(field, FLOOR_LEVEL)
    return (field, flow_scaling)


def solution(mesh):
    placed = (
        P("cls", "tiles", None),
        P("cls", "tiles", None),
        P("cls", "tiles", None),
        P(),
        P("cls"),
    )
    return jax.shard_map(
        on_device,
        mesh=mesh,
        in_specs=placed,
        out_specs=(P("cls", "tiles", None), P("cls", "tiles", None)),
        check_vma=False,
    )
```

profile of v0, /device:TPU:33, one launch (start us, length us, event | category | flops | bytes accessed | tf_op | source)
XLA Modules:
  0.0 441.5 jit_solution(72092592371518868)
XLA Ops:
  0.7 3.7 collective-permute-start.2
  7.6 3.6 collective-permute-start
  11.3 5.3 %collective-permute-start.1 = (f32[2,1,8192]{2,0,1:T(2,128)S(1)}, f32[2,1,8192]{2,0,1:T(2,128)S(1)}, u32[]{:S(2)}, u32[]{:S(2)}) collective-permute-start(f32[2,1,8192]{2,0,1:T(2,128)S(1)} %copy.194), channel_id=1, source_target_pairs={{2,0},{4,2},{6,4},{8,6},{10,8},{12,10},{14,12},{16,14},{18,16},{20... | collective-permute-start | bytes 196616 | tf_op jit(solution)/shard_map/ppermute | solution.py:36
  19.2 51.8 %reshape.59 = f32[2,4,4,2048,4]{4,3,2,1,0:T(8,128)} reshape(f32[2,16,8192]{2,1,0:T(8,128)} %param.7) | data formatting | bytes 2097152 | tf_op jit(solution)/shard_map/reshape | solution.py:94
  71.0 12.2 %reduce_sum.28 = f32[2,4,2048]{2,1,0:T(4,128)S(1)} reduce(f32[2,4,4,2048,4]{4,3,2,1,0:T(8,128)} %reshape.59, f32[]{:T(128)} %constant.54.clone.1), dimensions={2,4}, to_apply=%region_1.2 | reduce | flops 245760 | bytes 1114116 | tf_op jit(solution)/shard_map/reduce_sum | solution.py:95
  85.0 8.2 %collective-permute-start.11 = (f32[2,1,2048]{2,1,0:T(1,128)}, f32[2,1,2048]{2,1,0:T(1,128)S(1)}, u32[]{:S(2)}, u32[]{:S(2)}) collective-permute-start(f32[2,1,2048]{2,1,0:T(1,128)} %broadcast.163), channel_id=1, source_target_pairs={{2,0},{4,2},{6,4},{8,6},{10,8},{12,10},{14,12},{16,14},{18,16},{20... | collective-permute-start | bytes 49160 | tf_op jit(solution)/shard_map/ppermute | solution.py:36
  96.0 8.2 %collective-permute-start.9 = (f32[2,1,2048]{2,1,0:T(1,128)}, f32[2,1,2048]{2,1,0:T(1,128)S(1)}, u32[]{:S(2)}, u32[]{:S(2)}) collective-permute-start(f32[2,1,2048]{2,1,0:T(1,128)} %get-tuple-element.41), channel_id=1, source_target_pairs={{2,0},{4,2},{6,4},{8,6},{10,8},{12,10},{14,12},{16,14},{18,16},{20... | collective-permute-start | bytes 49160 | tf_op jit(solution)/shard_map/ppermute | solution.py:36
  106.5 2.8 broadcast_multiply_fusion.1
  111.4 8.3 %collective-permute-start.5 = (f32[2,1,8192]{2,0,1:T(2,128)S(1)}, f32[2,1,8192]{2,0,1:T(2,128)S(1)}, u32[]{:S(2)}, u32[]{:S(2)}) collective-permute-start(f32[2,1,8192]{2,0,1:T(2,128)S(1)} %copy.168), channel_id=1, source_target_pairs={{2,0},{4,2},{6,4},{8,6},{10,8},{12,10},{14,12},{16,14},{18,16},{20... | collective-permute-start | bytes 196616 | tf_op jit(solution)/shard_map/ppermute | solution.py:36
  121.3 4.1 broadcast_multiply_fusion
  127.5 9.2 %collective-permute-start.7 = (f32[2,1,8192]{2,0,1:T(2,128)S(1)}, f32[2,1,8192]{2,0,1:T(2,128)S(1)}, u32[]{:S(2)}, u32[]{:S(2)}) collective-permute-start(f32[2,1,8192]{2,0,1:T(2,128)S(1)} %copy.174), channel_id=1, source_target_pairs={{2,0},{4,2},{6,4},{8,6},{10,8},{12,10},{14,12},{16,14},{18,16},{20... | collective-permute-start | bytes 196616 | tf_op jit(solution)/shard_map/ppermute | solution.py:36
  139.3 3.7 fusion.49
  143.0 51.8 %reshape.58 = f32[2,4,4,2048,4]{4,3,2,1,0:T(8,128)} reshape(f32[2,16,8192]{2,1,0:T(8,128)} %fusion.49) | data formatting | bytes 2097152 | tf_op jit(solution)/shard_map/reshape | solution.py:99
  194.7 12.2 %reduce_sum.27 = f32[2,4,2048]{2,1,0:T(4,128)S(1)} reduce(f32[2,4,4,2048,4]{4,3,2,1,0:T(8,128)} %reshape.58, f32[]{:T(128)} %constant.54.clone.1), dimensions={2,4}, to_apply=%region_0.1 | reduce | flops 245760 | bytes 1114116 | tf_op jit(solution)/shard_map/reduce_sum | solution.py:100
  210.9 8.4 %collective-permute-start.13 = (f32[2,1,2048]{2,1,0:T(1,128)S(1)}, f32[2,1,2048]{2,1,0:T(1,128)S(1)}, u32[]{:S(2)}, u32[]{:S(2)}) collective-permute-start(f32[2,1,2048]{2,1,0:T(1,128)S(1)} %get-tuple-element.39), channel_id=1, source_target_pairs={{2,0},{4,2},{6,4},{8,6},{10,8},{12,10},{14,12},{16,14},{18,16},{20... | collective-permute-start | bytes 49160 | tf_op jit(solution)/shard_map/ppermute | solution.py:36
  223.4 9.0 %collective-permute-start.15 = (f32[2,1,2048]{2,1,0:T(1,128)S(1)}, f32[2,1,2048]{2,1,0:T(1,128)S(1)}, u32[]{:S(2)}, u32[]{:S(2)}) collective-permute-start(f32[2,1,2048]{2,1,0:T(1,128)S(1)} %get-tuple-element.37), channel_id=1, source_target_pairs={{2,0},{4,2},{6,4},{8,6},{10,8},{12,10},{14,12},{16,14},{18,16},{20... | collective-permute-start | bytes 49160 | tf_op jit(solution)/shard_map/ppermute | solution.py:36
  235.6 8.8 %collective-permute-start.17 = (f32[2,1,2048]{2,1,0:T(1,128)S(1)}, f32[2,1,2048]{2,1,0:T(1,128)S(1)}, u32[]{:S(2)}, u32[]{:S(2)}) collective-permute-start(f32[2,1,2048]{2,1,0:T(1,128)S(1)} %get-tuple-element.35), channel_id=1, source_target_pairs={{2,0},{4,2},{6,4},{8,6},{10,8},{12,10},{14,12},{16,14},{18,16},{20... | collective-permute-start | bytes 49160 | tf_op jit(solution)/shard_map/ppermute | solution.py:36
  247.7 8.8 %collective-permute-start.19 = (f32[2,1,2048]{2,1,0:T(1,128)S(1)}, f32[2,1,2048]{2,1,0:T(1,128)S(1)}, u32[]{:S(2)}, u32[]{:S(2)}) collective-permute-start(f32[2,1,2048]{2,1,0:T(1,128)S(1)} %get-tuple-element.33), channel_id=1, source_target_pairs={{2,0},{4,2},{6,4},{8,6},{10,8},{12,10},{14,12},{16,14},{18,16},{20... | collective-permute-start | bytes 49160 | tf_op jit(solution)/shard_map/ppermute | solution.py:36
  259.8 8.8 %collective-permute-start.21 = (f32[2,1,2048]{2,1,0:T(1,128)S(1)}, f32[2,1,2048]{2,1,0:T(1,128)S(1)}, u32[]{:S(2)}, u32[]{:S(2)}) collective-permute-start(f32[2,1,2048]{2,1,0:T(1,128)S(1)} %get-tuple-element.31), channel_id=1, source_target_pairs={{2,0},{4,2},{6,4},{8,6},{10,8},{12,10},{14,12},{16,14},{18,16},{20... | collective-permute-start | bytes 49160 | tf_op jit(solution)/shard_map/ppermute | solution.py:36
  272.0 8.8 %collective-permute-start.23 = (f32[2,1,2048]{2,1,0:T(1,128)S(1)}, f32[2,1,2048]{2,1,0:T(1,128)S(1)}, u32[]{:S(2)}, u32[]{:S(2)}) collective-permute-start(f32[2,1,2048]{2,1,0:T(1,128)S(1)} %get-tuple-element.29), channel_id=1, source_target_pairs={{2,0},{4,2},{6,4},{8,6},{10,8},{12,10},{14,12},{16,14},{18,16},{20... | collective-permute-start | bytes 49160 | tf_op jit(solution)/shard_map/ppermute | solution.py:36
  284.1 8.8 %collective-permute-start.25 = (f32[2,1,2048]{2,1,0:T(1,128)S(1)}, f32[2,1,2048]{2,1,0:T(1,128)S(1)}, u32[]{:S(2)}, u32[]{:S(2)}) collective-permute-start(f32[2,1,2048]{2,1,0:T(1,128)S(1)} %get-tuple-element.27), channel_id=1, source_target_pairs={{2,0},{4,2},{6,4},{8,6},{10,8},{12,10},{14,12},{16,14},{18,16},{20... | collective-permute-start | bytes 49160 | tf_op jit(solution)/shard_map/ppermute | solution.py:36
  294.5 1.9 copy.179
  296.4 5.8 %broadcast_in_dim.28 = f32[2,16,2048,4]{1,3,2,0:T(4,128)} broadcast(f32[2,16,2048]{1,2,0:T(8,128)} %copy.179), dimensions={0,1,2} | broadcast | bytes 1310720 | tf_op jit(solution)/shard_map/broadcast_in_dim | solution.py:104
  302.3 6.0 %copy.180 = f32[2,16,8192]{2,1,0:T(8,128)} copy(f32[2,16,8192]{1,2,0:T(8,128)} %bitcast.4) | data formatting | bytes 2097152 | tf_op jit(solution)/shard_map/reshape | solution.py:104
  313.0 8.8 %collective-permute-start.27 = (f32[2,1,8192]{2,0,1:T(2,128)S(1)}, f32[2,1,8192]{2,0,1:T(2,128)}, u32[]{:S(2)}, u32[]{:S(2)}) collective-permute-start(f32[2,1,8192]{2,0,1:T(2,128)S(1)} %copy.183), channel_id=1, source_target_pairs={{2,0},{4,2},{6,4},{8,6},{10,8},{12,10},{14,12},{16,14},{18,16},{20... | collective-permute-start | bytes 196616 | tf_op jit(solution)/shard_map/ppermute | solution.py:36
  321.8 2.1 reduce_sum.29
  323.9 97.9 %psum.7 = f32[]{:T(128)} all-reduce(f32[]{:T(128)} %reduce_sum.29), channel_id=1, replica_groups=mesh['tiles'=128,'cls'=2] {'tiles','cls'}, use_global_device_ids=true, to_apply=%region_3.4 | all-reduce | flops 1 | bytes 8 | tf_op jit(solution)/shard_map/psum | solution.py:122
  422.9 2.0 select_maximum_fusion.2
  425.0 3.2 fusion.73
  428.4 2.2 collective-permute-start.28
  430.6 3.0 collective-permute-start.29
  437.1 4.4 maximum_divide_fusion
  (147 shorter events, 56.3 us)
Async XLA Ops:
  0.7 95.4 %collective-permute-start.2 = (f32[2,1,8192]{2,0,1:T(2,128)S(1)}, f32[2,1,8192]{2,0,1:T(2,128)}, u32[]{:S(2)}, u32[]{:S(2)}) collective-permute-start(f32[2,1,8192]{2,0,1:T(2,128)S(1)} %broadcast.156), channel_id=1, source_target_pairs={{0,2},{2,4},{4,6},{6,8},{8,10},{10,12},{12,14},{14,16},{16,18},{18... | collective-permute-start | bytes 196616 | tf_op jit(solution)/shard_map/ppermute | solution.py:35
  4.3 100.8 %collective-permute-start.3 = (f32[2,1,8192]{2,0,1:T(2,128)S(1)}, f32[2,1,8192]{2,0,1:T(2,128)S(1)}, u32[]{:S(2)}, u32[]{:S(2)}) collective-permute-start(f32[2,1,8192]{2,0,1:T(2,128)S(1)} %broadcast.156), channel_id=1, source_target_pairs={{2,0},{4,2},{6,4},{8,6},{10,8},{12,10},{14,12},{16,14},{18,16},{20... | collective-permute-start | bytes 196616 | tf_op jit(solution)/shard_map/ppermute | solution.py:36
  7.6 77.3 %collective-permute-start = (f32[2,1,8192]{2,0,1:T(2,128)S(1)}, f32[2,1,8192]{2,0,1:T(2,128)S(1)}, u32[]{:S(2)}, u32[]{:S(2)}) collective-permute-start(f32[2,1,8192]{2,0,1:T(2,128)S(1)} %copy.193), channel_id=1, source_target_pairs={{0,2},{2,4},{4,6},{6,8},{8,10},{10,12},{12,14},{14,16},{16,18},{18... | collective-permute-start | bytes 196616 | tf_op jit(solution)/shard_map/ppermute | solution.py:35
  11.3 81.9 %collective-permute-start.1 = (f32[2,1,8192]{2,0,1:T(2,128)S(1)}, f32[2,1,8192]{2,0,1:T(2,128)S(1)}, u32[]{:S(2)}, u32[]{:S(2)}) collective-permute-start(f32[2,1,8192]{2,0,1:T(2,128)S(1)} %copy.194), channel_id=1, source_target_pairs={{2,0},{4,2},{6,4},{8,6},{10,8},{12,10},{14,12},{16,14},{18,16},{20... | collective-permute-start | bytes 196616 | tf_op jit(solution)/shard_map/ppermute | solution.py:36
  17.3 119.4 %collective-permute-start.10 = (f32[2,1,2048]{2,1,0:T(1,128)}, f32[2,1,2048]{2,1,0:T(1,128)}, u32[]{:S(2)}, u32[]{:S(2)}) collective-permute-start(f32[2,1,2048]{2,1,0:T(1,128)} %broadcast.163), channel_id=1, source_target_pairs={{0,2},{2,4},{4,6},{6,8},{8,10},{10,12},{12,14},{14,16},{16,18},{18... | collective-permute-start | bytes 49160 | tf_op jit(solution)/shard_map/ppermute | solution.py:35
  85.0 51.8 %collective-permute-start.11 = (f32[2,1,2048]{2,1,0:T(1,128)}, f32[2,1,2048]{2,1,0:T(1,128)S(1)}, u32[]{:S(2)}, u32[]{:S(2)}) collective-permute-start(f32[2,1,2048]{2,1,0:T(1,128)} %broadcast.163), channel_id=1, source_target_pairs={{2,0},{4,2},{6,4},{8,6},{10,8},{12,10},{14,12},{16,14},{18,16},{20... | collective-permute-start | bytes 49160 | tf_op jit(solution)/shard_map/ppermute | solution.py:36
  93.2 18.2 %collective-permute-start.8 = (f32[2,1,2048]{2,1,0:T(1,128)}, f32[2,1,2048]{2,1,0:T(1,128)S(1)}, u32[]{:S(2)}, u32[]{:S(2)}) collective-permute-start(f32[2,1,2048]{2,1,0:T(1,128)} %get-tuple-element.40), channel_id=1, source_target_pairs={{0,2},{2,4},{4,6},{6,8},{8,10},{10,12},{12,14},{14,16},{16,18},{18... | collective-permute-start | bytes 49160 | tf_op jit(solution)/shard_map/ppermute | solution.py:35
  96.0 23.8 %collective-permute-start.9 = (f32[2,1,2048]{2,1,0:T(1,128)}, f32[2,1,2048]{2,1,0:T(1,128)S(1)}, u32[]{:S(2)}, u32[]{:S(2)}) collective-permute-start(f32[2,1,2048]{2,1,0:T(1,128)} %get-tuple-element.41), channel_id=1, source_target_pairs={{2,0},{4,2},{6,4},{8,6},{10,8},{12,10},{14,12},{16,14},{18,16},{20... | collective-permute-start | bytes 49160 | tf_op jit(solution)/shard_map/ppermute | solution.py:36
  109.4 10.5 %collective-permute-start.4 = (f32[2,1,8192]{2,0,1:T(2,128)S(1)}, f32[2,1,8192]{2,0,1:T(2,128)S(1)}, u32[]{:S(2)}, u32[]{:S(2)}) collective-permute-start(f32[2,1,8192]{2,0,1:T(2,128)S(1)} %copy.166), channel_id=1, source_target_pairs={{0,2},{2,4},{4,6},{6,8},{8,10},{10,12},{12,14},{14,16},{16,18},{18... | collective-permute-start | bytes 196616 | tf_op jit(solution)/shard_map/ppermute | solution.py:35
  111.4 9.0 %collective-permute-start.5 = (f32[2,1,8192]{2,0,1:T(2,128)S(1)}, f32[2,1,8192]{2,0,1:T(2,128)S(1)}, u32[]{:S(2)}, u32[]{:S(2)}) collective-permute-start(f32[2,1,8192]{2,0,1:T(2,128)S(1)} %copy.168), channel_id=1, source_target_pairs={{2,0},{4,2},{6,4},{8,6},{10,8},{12,10},{14,12},{16,14},{18,16},{20... | collective-permute-start | bytes 196616 | tf_op jit(solution)/shard_map/ppermute | solution.py:36
  125.6 12.8 %collective-permute-start.6 = (f32[2,1,8192]{2,0,1:T(2,128)S(1)}, f32[2,1,8192]{2,0,1:T(2,128)S(1)}, u32[]{:S(2)}, u32[]{:S(2)}) collective-permute-start(f32[2,1,8192]{2,0,1:T(2,128)S(1)} %copy.172), channel_id=1, source_target_pairs={{0,2},{2,4},{4,6},{6,8},{8,10},{10,12},{12,14},{14,16},{16,18},{18... | collective-permute-start | bytes 196616 | tf_op jit(solution)/shard_map/ppermute | solution.py:35
  127.5 10.9 %collective-permute-start.7 = (f32[2,1,8192]{2,0,1:T(2,128)S(1)}, f32[2,1,8192]{2,0,1:T(2,128)S(1)}, u32[]{:S(2)}, u32[]{:S(2)}) collective-permute-start(f32[2,1,8192]{2,0,1:T(2,128)S(1)} %copy.174), channel_id=1, source_target_pairs={{2,0},{4,2},{6,4},{8,6},{10,8},{12,10},{14,12},{16,14},{18,16},{20... | collective-permute-start | bytes 196616 | tf_op jit(solution)/shard_map/ppermute | solution.py:36
  209.0 10.3 %collective-permute-start.12 = (f32[2,1,2048]{2,1,0:T(1,128)S(1)}, f32[2,1,2048]{2,1,0:T(1,128)S(1)}, u32[]{:S(2)}, u32[]{:S(2)}) collective-permute-start(f32[2,1,2048]{2,1,0:T(1,128)S(1)} %get-tuple-element.38), channel_id=1, source_target_pairs={{0,2},{2,4},{4,6},{6,8},{8,10},{10,12},{12,14},{14,16},{16,18},{18... | collective-permute-start | bytes 49160 | tf_op jit(solution)/shard_map/ppermute | solution.py:35
  210.9 9.2 %collective-permute-start.13 = (f32[2,1,2048]{2,1,0:T(1,128)S(1)}, f32[2,1,2048]{2,1,0:T(1,128)S(1)}, u32[]{:S(2)}, u32[]{:S(2)}) collective-permute-start(f32[2,1,2048]{2,1,0:T(1,128)S(1)} %get-tuple-element.39), channel_id=1, source_target_pairs={{2,0},{4,2},{6,4},{8,6},{10,8},{12,10},{14,12},{16,14},{18,16},{20... | collective-permute-start | bytes 49160 | tf_op jit(solution)/shard_map/ppermute | solution.py:36
  221.4 11.0 %collective-permute-start.14 = (f32[2,1,2048]{2,1,0:T(1,128)S(1)}, f32[2,1,2048]{2,1,0:T(1,128)S(1)}, u32[]{:S(2)}, u32[]{:S(2)}) collective-permute-start(f32[2,1,2048]{2,1,0:T(1,128)S(1)} %get-tuple-element.36), channel_id=1, source_target_pairs={{0,2},{2,4},{4,6},{6,8},{8,10},{10,12},{12,14},{14,16},{16,18},{18... | collective-permute-start | bytes 49160 | tf_op jit(solution)/shard_map/ppermute | solution.py:35
  223.4 9.6 %collective-permute-start.15 = (f32[2,1,2048]{2,1,0:T(1,128)S(1)}, f32[2,1,2048]{2,1,0:T(1,128)S(1)}, u32[]{:S(2)}, u32[]{:S(2)}) collective-permute-start(f32[2,1,2048]{2,1,0:T(1,128)S(1)} %get-tuple-element.37), channel_id=1, source_target_pairs={{2,0},{4,2},{6,4},{8,6},{10,8},{12,10},{14,12},{16,14},{18,16},{20... | collective-permute-start | bytes 49160 | tf_op jit(solution)/shard_map/ppermute | solution.py:36
  233.6 10.7 %collective-permute-start.16 = (f32[2,1,2048]{2,1,0:T(1,128)S(1)}, f32[2,1,2048]{2,1,0:T(1,128)S(1)}, u32[]{:S(2)}, u32[]{:S(2)}) collective-permute-start(f32[2,1,2048]{2,1,0:T(1,128)S(1)} %get-tuple-element.34), channel_id=1, source_target_pairs={{0,2},{2,4},{4,6},{6,8},{8,10},{10,12},{12,14},{14,16},{16,18},{18... | collective-permute-start | bytes 49160 | tf_op jit(solution)/shard_map/ppermute | solution.py:35
  235.6 9.6 %collective-permute-start.17 = (f32[2,1,2048]{2,1,0:T(1,128)S(1)}, f32[2,1,2048]{2,1,0:T(1,128)S(1)}, u32[]{:S(2)}, u32[]{:S(2)}) collective-permute-start(f32[2,1,2048]{2,1,0:T(1,128)S(1)} %get-tuple-element.35), channel_id=1, source_target_pairs={{2,0},{4,2},{6,4},{8,6},{10,8},{12,10},{14,12},{16,14},{18,16},{20... | collective-permute-start | bytes 49160 | tf_op jit(solution)/shard_map/ppermute | solution.py:36
  245.8 10.7 %collective-permute-start.18 = (f32[2,1,2048]{2,1,0:T(1,128)S(1)}, f32[2,1,2048]{2,1,0:T(1,128)S(1)}, u32[]{:S(2)}, u32[]{:S(2)}) collective-permute-start(f32[2,1,2048]{2,1,0:T(1,128)S(1)} %get-tuple-element.32), channel_id=1, source_target_pairs={{0,2},{2,4},{4,6},{6,8},{8,10},{10,12},{12,14},{14,16},{16,18},{18... | collective-permute-start | bytes 49160 | tf_op jit(solution)/shard_map/ppermute | solution.py:35
  247.7 9.6 %collective-permute-start.19 = (f32[2,1,2048]{2,1,0:T(1,128)S(1)}, f32[2,1,2048]{2,1,0:T(1,128)S(1)}, u32[]{:S(2)}, u32[]{:S(2)}) collective-permute-start(f32[2,1,2048]{2,1,0:T(1,128)S(1)} %get-tuple-element.33), channel_id=1, source_target_pairs={{2,0},{4,2},{6,4},{8,6},{10,8},{12,10},{14,12},{16,14},{18,16},{20... | collective-permute-start | bytes 49160 | tf_op jit(solution)/shard_map/ppermute | solution.py:36
  257.9 10.7 %collective-permute-start.20 = (f32[2,1,2048]{2,1,0:T(1,128)S(1)}, f32[2,1,2048]{2,1,0:T(1,128)S(1)}, u32[]{:S(2)}, u32[]{:S(2)}) collective-permute-start(f32[2,1,2048]{2,1,0:T(1,128)S(1)} %get-tuple-element.30), channel_id=1, source_target_pairs={{0,2},{2,4},{4,6},{6,8},{8,10},{10,12},{12,14},{14,16},{16,18},{18... | collective-permute-start | bytes 49160 | tf_op jit(solution)/shard_map/ppermute | solution.py:35
  259.8 9.6 %collective-permute-start.21 = (f32[2,1,2048]{2,1,0:T(1,128)S(1)}, f32[2,1,2048]{2,1,0:T(1,128)S(1)}, u32[]{:S(2)}, u32[]{:S(2)}) collective-permute-start(f32[2,1,2048]{2,1,0:T(1,128)S(1)} %get-tuple-element.31), channel_id=1, source_target_pairs={{2,0},{4,2},{6,4},{8,6},{10,8},{12,10},{14,12},{16,14},{18,16},{20... | collective-permute-start | bytes 49160 | tf_op jit(solution)/shard_map/ppermute | solution.py:36
  270.1 10.7 %collective-permute-start.22 = (f32[2,1,2048]{2,1,0:T(1,128)S(1)}, f32[2,1,2048]{2,1,0:T(1,128)S(1)}, u32[]{:S(2)}, u32[]{:S(2)}) collective-permute-start(f32[2,1,2048]{2,1,0:T(1,128)S(1)} %get-tuple-element.28), channel_id=1, source_target_pairs={{0,2},{2,4},{4,6},{6,8},{8,10},{10,12},{12,14},{14,16},{16,18},{18... | collective-permute-start | bytes 49160 | tf_op jit(solution)/shard_map/ppermute | solution.py:35
  272.0 9.6 %collective-permute-start.23 = (f32[2,1,2048]{2,1,0:T(1,128)S(1)}, f32[2,1,2048]{2,1,0:T(1,128)S(1)}, u32[]{:S(2)}, u32[]{:S(2)}) collective-permute-start(f32[2,1,2048]{2,1,0:T(1,128)S(1)} %get-tuple-element.29), channel_id=1, source_target_pairs={{2,0},{4,2},{6,4},{8,6},{10,8},{12,10},{14,12},{16,14},{18,16},{20... | collective-permute-start | bytes 49160 | tf_op jit(solution)/shard_map/ppermute | solution.py:36
  282.2 10.7 %collective-permute-start.24 = (f32[2,1,2048]{2,1,0:T(1,128)S(1)}, f32[2,1,2048]{2,1,0:T(1,128)S(1)}, u32[]{:S(2)}, u32[]{:S(2)}) collective-permute-start(f32[2,1,2048]{2,1,0:T(1,128)S(1)} %get-tuple-element.26), channel_id=1, source_target_pairs={{0,2},{2,4},{4,6},{6,8},{8,10},{10,12},{12,14},{14,16},{16,18},{18... | collective-permute-start | bytes 49160 | tf_op jit(solution)/shard_map/ppermute | solution.py:35
  284.1 9.6 %collective-permute-start.25 = (f32[2,1,2048]{2,1,0:T(1,128)S(1)}, f32[2,1,2048]{2,1,0:T(1,128)S(1)}, u32[]{:S(2)}, u32[]{:S(2)}) collective-permute-start(f32[2,1,2048]{2,1,0:T(1,128)S(1)} %get-tuple-element.27), channel_id=1, source_target_pairs={{2,0},{4,2},{6,4},{8,6},{10,8},{12,10},{14,12},{16,14},{18,16},{20... | collective-permute-start | bytes 49160 | tf_op jit(solution)/shard_map/ppermute | solution.py:36
  311.0 110.8 %collective-permute-start.26 = (f32[2,1,8192]{2,0,1:T(2,128)S(1)}, f32[2,1,8192]{2,0,1:T(2,128)S(1)}, u32[]{:S(2)}, u32[]{:S(2)}) collective-permute-start(f32[2,1,8192]{2,0,1:T(2,128)S(1)} %copy.181), channel_id=1, source_target_pairs={{0,2},{2,4},{4,6},{6,8},{8,10},{10,12},{12,14},{14,16},{16,18},{18... | collective-permute-start | bytes 196616 | tf_op jit(solution)/shard_map/ppermute | solution.py:35
  313.0 108.8 %collective-permute-start.27 = (f32[2,1,8192]{2,0,1:T(2,128)S(1)}, f32[2,1,8192]{2,0,1:T(2,128)}, u32[]{:S(2)}, u32[]{:S(2)}) collective-permute-start(f32[2,1,8192]{2,0,1:T(2,128)S(1)} %copy.183), channel_id=1, source_target_pairs={{2,0},{4,2},{6,4},{8,6},{10,8},{12,10},{14,12},{16,14},{18,16},{20... | collective-permute-start | bytes 196616 | tf_op jit(solution)/shard_map/ppermute | solution.py:36
  323.9 101.0 %copy-start.7 = (f32[2,1,8192]{2,1,0:T(1,128)S(1)}, f32[2,1,8192]{2,1,0:T(1,128)}, u32[]{:S(2)}) copy-start(f32[2,1,8192]{2,1,0:T(1,128)} %copy-done.6) | copy-start | bytes 196612
  323.9 101.0 %copy-start.9 = (f32[2,1,8192]{2,1,0:T(1,128)S(1)}, f32[2,1,8192]{2,1,0:T(1,128)}, u32[]{:S(2)}) copy-start(f32[2,1,8192]{2,1,0:T(1,128)} %copy-done.8) | copy-start | bytes 196612
  428.4 5.9 %collective-permute-start.28 = (f32[2,1,8192]{2,0,1:T(2,128)S(1)}, f32[2,1,8192]{2,0,1:T(2,128)S(1)}, u32[]{:S(2)}, u32[]{:S(2)}) collective-permute-start(f32[2,1,8192]{2,0,1:T(2,128)S(1)} %copy.187), channel_id=1, source_target_pairs={{0,2},{2,4},{4,6},{6,8},{8,10},{10,12},{12,14},{14,16},{16,18},{18... | collective-permute-start | bytes 196616 | tf_op jit(solution)/shard_map/ppermute | solution.py:35
  430.6 5.6 %collective-permute-start.29 = (f32[2,1,8192]{2,0,1:T(2,128)S(1)}, f32[2,1,8192]{2,0,1:T(2,128)S(1)}, u32[]{:S(2)}, u32[]{:S(2)}) collective-permute-start(f32[2,1,8192]{2,0,1:T(2,128)S(1)} %copy.189), channel_id=1, source_target_pairs={{2,0},{4,2},{6,4},{8,6},{10,8},{12,10},{14,12},{16,14},{18,16},{20... | collective-permute-start | bytes 196616 | tf_op jit(solution)/shard_map/ppermute | solution.py:36
  (13 other events, 171.2 us)
where the time goes:
time: 450 us; the launch traced here: 441 us
  starting transfers between devices  147 us (33%)
  local copies, waits for them, and re-layouts  126 us (28%)
  blocking collectives  97.9 us (22%)
  other arithmetic  61.3 us (14%)
  waiting for transfers between devices  7.72 us (2%)
    ppermute x15, starting transfers between devices, with_halo(): after = lax.ppermute(leading, axis, down)  114 us
    psum x1, blocking collectives, on_device(): global_mass = lax.psum(jnp.sum(source), ('tiles', 'cls'))  97.9 us
    reshape x1, local copies, waits for them, and re-layouts, block_mean(): field.reshape(field.shape[0], field.shape[1] // 4, 4, field.shape[2] // 4...  51.8 us
    reshape x1, local copies, waits for them, and re-layouts, block_sum(): field.reshape(field.shape[0], field.shape[1] // 4, 4, field.shape[2] // 4...  51.8 us
    ppermute x15, starting transfers between devices, with_halo(): before = lax.ppermute(last, axis, up)  32.5 us
    mul x11, other arithmetic, jacobi(): land_cells * (center + OMEGA_DAMP * (right_side - applied) / coeffs[2])  15.6 us
    reduce_sum x1, other arithmetic, block_mean(): return jnp.mean(shaped, axis=(2, 4))  12.2 us
    reduce_sum x1, other arithmetic, block_sum(): return jnp.sum(shaped, axis=(2, 4))  12.2 us
  transfers between devices with their start and end apart: 30, of which 9 were waited for; matrix products, arithmetic and copies ran while one was open for 19% of the time, Pallas kernels for 0%

commit v1 on v0

v1 whole, which is shorter than its diff:
```python
import jax
import jax.numpy as jnp
from jax import lax
from jax.experimental import pallas as pl
from jax.experimental.pallas import tpu as pltpu
from jax.sharding import PartitionSpec as P

MESH = pl.DeviceIdType.MESH
F32 = jnp.float32
BF16 = jnp.bfloat16
FLOOR_LEVEL = 0.25
TS = 256


def kernel(
    ntiles, ncls,
    mask_ref, target_ref, b_in, src_in, k_in,
    heat_out, flow_out,
    KN, BN, SN, KHN, BHN, KL, CL, WL, DG, FL, GL, KH, CH, WH, FH, GH, RS, CK, GQ, ICK, PC, QC, UC, UP, OH, OF, MS, MR,
    sem_in, sem_out, k_send, k_recv, b_send, b_recv, q_send, q_recv, p_send, p_recv, m_send, m_recv,
):
    me = lax.axis_index("tiles")
    cl = lax.axis_index("cls")
    has_prev, has_next = me > 0, me < ntiles - 1
    has_prev2, has_next2 = me > 1, me < ntiles - 2

    sub = lax.broadcasted_iota(jnp.int32, (8, 128), 0)
    lane = lax.broadcasted_iota(jnp.int32, (8, 128), 1)
    s4 = sub & 3
    m0, m3 = s4 == 0, s4 == 3
    half0 = s4 < 2
    side0 = (sub & 1) == 0
    lane0, lane127 = lane == 0, lane == 127
    zero = jnp.zeros((8, 128), F32)

    def rs(x, n):
        return pltpu.roll(x, n % 8, 0)

    def rl(x, n):
        return pltpu.roll(x, n % 128, 1)

    def load_copies(hbm, vmem, base, s):
        return [
            pltpu.make_async_copy(
                hbm.at[c, rt], vmem.at[pl.ds(base, 64), pl.ds(16 * c + 8 * rt, 8), :], sem_in.at[s * 4 + 2 * c + rt]
            )
            for c in range(2)
            for rt in range(2)
        ]

    k_loads = load_copies(k_in, KN, 1, 0)
    b_loads = load_copies(b_in, BN, 0, 1)
    s_loads = load_copies(src_in, SN, 0, 2)
    for copy in k_loads + s_loads + b_loads:
        copy.start()

    low = me % 8
    mid = me // 8 % 2
    high = me // 16
    place = 2 * mid + cl

    def mass_peer(stage, r):
        if stage == 0:
            return {"tiles": me - low + (low + r) % 8, "cls": cl}
        if stage == 1:
            other = (place + r) % 4
            return {"tiles": me + 8 * (other // 2 - mid), "cls": other % 2}
        return {"tiles": me + 16 * ((high + r) % 8 - high), "cls": cl}

    sizes = (8, 4, 8)
    starts = (0, 8, 12)

    barrier = pltpu.get_barrier_semaphore()

    def greet(there):
        pl.semaphore_signal(barrier, inc=1, device_id=there, device_id_type=MESH)

    for step, there in ((-1, has_prev), (1, has_next), (-2, has_prev2), (2, has_next2)):
        @pl.when(there)
        def _():
            greet({"tiles": me + step})
    for stage in range(3):
        for r in range(1, sizes[stage]):
            greet(mass_peer(stage, r))
    one = jnp.int32(1)
    nil = jnp.int32(0)
    greeted = 17
    for there in (has_prev, has_next, has_prev2, has_next2):
        greeted = greeted + jnp.where(there, one, nil)
    pl.semaphore_wait(barrier, greeted)

    def halo_copies(hbm, vmem, base, send, recv):
        to_next, to_prev = [], []
        for c in range(2):
            for half in range(2):
                n = 2 * c + half
                to_next.append(pltpu.make_async_remote_copy(
                    src_ref=hbm.at[c, 1, pl.ds(32 * half, 32), pl.ds(4, 4), :],
                    dst_ref=vmem.at[pl.ds(base, 32), pl.ds(16 * c + 8 * half, 4), :],
                    send_sem=send.at[n], recv_sem=recv.at[n],
                    device_id={"tiles": me + 1}, device_id_type=MESH))
                to_prev.append(pltpu.make_async_remote_copy(
                    src_ref=hbm.at[c, 0, pl.ds(32 * half, 32), pl.ds(0, 4), :],
                    dst_ref=vmem.at[pl.ds(base, 32), pl.ds(16 * c + 8 * half + 4, 4), :],
                    send_sem=send.at[4 + n], recv_sem=recv.at[4 + n],
                    device_id={"tiles": me - 1}, device_id_type=MESH))
        return to_next, to_prev

    k_next, k_prev = halo_copies(k_in, KHN, 1, k_send, k_recv)
    b_next, b_prev = halo_copies(b_in, BHN, 0, b_send, b_recv)

    def start_all(copies, there):
        @pl.when(there)
        def _():
            for copy in copies:
                copy.start()

    def recv_all(copies, there):
        @pl.when(there)
        def _():
            for copy in copies:
                copy.wait_recv()

    def sent_all(copies, there):
        @pl.when(there)
        def _():
            for copy in copies:
                copy.wait_send()

    start_all(k_next, has_next)
    start_all(k_prev, has_prev)
    start_all(b_next, has_next)
    start_all(b_prev, has_prev)

    for n in (0, 65):
        KN[n] = jnp.zeros((32, 128), F32)
        for t in range(4):
            KL[n, t] = zero
            CL[n, t] = zero
            FL[n, t] = zero
            GL[n, t] = zero

    def outside(first, there):
        @pl.when(jnp.logical_not(there))
        def _():
            for c in range(2):
                for half in range(2):
                    row = 16 * c + 8 * half + first
                    KHN[pl.ds(1, 32), pl.ds(row, 4), :] = jnp.zeros((32, 4, 128), F32)
                    BHN[pl.ds(0, 32), pl.ds(row, 4), :] = jnp.zeros((32, 4, 128), F32)

    outside(0, has_prev)
    outside(4, has_next)

    def clear(slot, there):
        @pl.when(jnp.logical_not(there))
        def _():
            PC[slot] = jnp.zeros((16, 8, 128), F32)
            QC[slot] = jnp.zeros((16, 8, 128), F32)

    clear(0, has_prev2)
    clear(1, has_prev)
    clear(3, has_next)
    clear(4, has_next2)
    for q in (0, 17):
        for slot in range(5):
            UC[q, slot] = zero
            UP[q, slot] = zero
        CK[q] = zero

    def mass_copy(stage, r):
        return pltpu.make_async_remote_copy(
            src_ref=MS.at[stage], dst_ref=MR.at[starts[stage] + r],
            send_sem=m_send.at[starts[stage] + r], recv_sem=m_recv.at[starts[stage] + r],
            device_id=mass_peer(stage, r), device_id_type=MESH)

    def mass_start(stage):
        for r in range(1, sizes[stage]):
            mass_copy(stage, r).start()

    def mass_total(stage):
        total = MS[stage]
        for r in range(1, sizes[stage]):
            mass_copy(stage, r).wait_recv()
        for r in range(1, sizes[stage]):
            total = total + MR[starts[stage] + r]
        return total

    for copy in s_loads:
        copy.wait()

    def add_source(n, sums):
        return tuple(
            sums[i] + SN[n * 2 + i // 4, pl.ds(8 * (i % 4), 8), :] for i in range(8)
        )

    sums = lax.fori_loop(0, 32, add_source, (zero,) * 8)
    total = sums[0]
    for part in sums[1:]:
        total = total + part
    MS[0] = total
    mass_start(0)

    row_tile = me * 16 // TS
    prev_tile = jnp.maximum(me * 16 - 1, 0) // TS
    next_tile = jnp.minimum(me * 16 + 16, ntiles * 16 - 1) // TS

    def land(row, block):
        return mask_ref[row, block // 2].astype(F32)

    def along(first, count, sa, finalize, carry, unroll):
        def body(n, carry):
            for i in range(unroll):
                j = first + n * unroll + i
                before, s, right, left = carry
                s_next, a_next = sa(j + 1)
                right_next = [rl(x, 1) for x in a_next]
                left_next = [rl(x, -1) for x in a_next]
                near = [
                    s[t] + jnp.where(lane0, before[t], right[t]) + jnp.where(lane127, left_next[t], left[t])
                    for t in range(len(s))
                ]
                finalize(j, i, near)
                carry = (right, s_next, right_next, left_next)
            return carry

        return lax.fori_loop(0, count // unroll, body, carry)

    def begin(sa, first):
        _, a_before = sa(first - 1)
        s, a = sa(first)
        return ([rl(x, 1) for x in a_before], s, [rl(x, 1) for x in a], [rl(x, -1) for x in a])

    def sums_of(u, up0, down3):
        s = [up0 + u[1], u[0] + u[2], u[1] + u[3], u[2] + down3]
        return s, [u[t] + 0.5 * s[t] for t in range(4)]

    def local_stage(u_at, edge_at, finalize, unroll=4):
        def sa_of(half):
            def sa(j):
                u = u_at(j + 1)
                h = j - 32 * half + 1
                above, below = edge_at(h, 3), edge_at(h, 0)
                if half == 0:
                    below = rs(below, 2)
                else:
                    above = rs(above, -2)
                return sums_of(
                    u, jnp.where(m0, above, rs(u[3], 1)), jnp.where(m3, below, rs(u[0], -1))
                )
            return sa

        carry = begin(sa_of(0), 0)
        carry = along(0, 32, sa_of(0), finalize, carry, unroll)
        along(32, 32, sa_of(1), finalize, carry, unroll)

    def halo_stage(u_at, local_at, finalize, unroll=4):
        def sa(j):
            u = u_at(j + 1)
            up0 = jnp.where(m3, local_at(j + 33, 3), rs(local_at(j + 1, 3), -2))
            down3 = jnp.where(m0, local_at(j + 1, 0), rs(local_at(j + 33, 0), 2))
            return sums_of(u, up0, down3)

        along(0, 32, sa, finalize, begin(sa, 0), unroll)

    def pad_halo(ref):
        for t in range(4):
            ref[0, t] = jnp.where(half0, 0.0, rs(ref[32, t], 2))
            ref[33, t] = jnp.where(half0, rs(ref[1, t], -2), 0.0)

    def tile_of(ref, n, t):
        return ref[n, pl.ds(t, 8, stride=4), :]

    fine_lane = lax.broadcasted_iota(jnp.int32, (512, 128), 0)
    coarse_lane = lax.broadcasted_iota(jnp.int32, (512, 128), 1)
    squeeze = jnp.where(fine_lane // 4 == coarse_lane, 1.0, 0.0).astype(BF16)
    fine_lane2 = lax.broadcasted_iota(jnp.int32, (128, 512), 1)
    coarse_lane2 = lax.broadcasted_iota(jnp.int32, (128, 512), 0)
    stretch = jnp.where(fine_lane2 // 4 == coarse_lane2, 1.0, 0.0).astype(BF16)

    def exact_dot(x, y):
        high = x.astype(BF16)
        rest = x - high.astype(F32)
        middle = rest.astype(BF16)
        low_part = (rest - middle.astype(F32)).astype(BF16)
        out = jnp.dot(high, y, preferred_element_type=F32)
        out = out + jnp.dot(middle, y, preferred_element_type=F32)
        return out + jnp.dot(low_part, y, preferred_element_type=F32)

    for copy in k_loads:
        copy.wait()

    def speed_body(q, _):
        for i in range(4):
            tiles = [tile_of(KN, 4 * q + i + 1, t) for t in range(4)]
            for t in range(4):
                KL[4 * q + i + 1, t] = tiles[t]
            RS[pl.ds(pl.multiple_of(q * 8, 8), 8), pl.ds(128 * i, 128)] = (tiles[0] + tiles[1]) + (tiles[2] + tiles[3])
        return 0

    lax.fori_loop(0, 16, speed_body, 0)
    CK[pl.ds(1, 16)] = (exact_dot(RS[...][:128], squeeze) * 0.0625).reshape(16, 8, 128)

    for copy in b_loads:
        copy.wait()
    recv_all(k_next, has_prev)
    recv_all(k_prev, has_next)

    def halo_speed(q, _):
        for i in range(4):
            tiles = [tile_of(KHN, 4 * q + i + 1, t) for t in range(4)]
            for t in range(4):
                KH[4 * q + i + 1, t] = tiles[t]
            RS[pl.ds(pl.multiple_of(q * 8, 8), 8), pl.ds(128 * i, 128)] = (tiles[0] + tiles[1]) + (tiles[2] + tiles[3])
        return 0

    lax.fori_loop(0, 8, halo_speed, 0)
    pad_halo(KH)
    ckh = (exact_dot(RS[pl.ds(0, 64), :], squeeze) * 0.0625).reshape(8, 8, 128)

    def coarse_sa(q):
        c = CK[q + 1]
        h = ckh[q % 8]
        if q < 8:
            above, below = h, rs(h, 2)
        else:
            above, below = rs(h, -2), h
        s = jnp.where(m0, above, rs(c, 1)) + jnp.where(m3, below, rs(c, -1))
        return s, c + 0.5 * s

    pairs = [coarse_sa(q) for q in range(16)]
    for q in range(16):
        c = CK[q + 1]
        left = rl(pairs[q][1], 1)
        left = jnp.where(lane0, rl(pairs[q - 1][1], 1) if q else 0.0, left)
        right = rl(pairs[q][1], -1)
        right = jnp.where(lane127, rl(pairs[q + 1][1], -1) if q < 15 else 0.0, right)
        near = pairs[q][0] + left + right
        land_q = jnp.where(lane < 64, land(row_tile, 4 * q), land(row_tile, 4 * q + 2))
        g = c * land_q / (16.0 + 32.0 * c * near)
        GQ[q] = g
        QC[2, q] = 25.6 * c * g
        ICK[q] = 1.0 / c
    for q in range(8):
        ICK[16 + q] = 1.0 / jnp.maximum(ckh[q], 1e-30)

    def coarse_copies(ref, send, recv):
        out = []
        for n, (step, there, back) in enumerate(
            ((1, has_next, has_prev), (-1, has_prev, has_next), (2, has_next2, has_prev2), (-2, has_prev2, has_next2))
        ):
            out.append((pltpu.make_async_remote_copy(
                src_ref=ref.at[2], dst_ref=ref.at[2 - step],
                send_sem=send.at[n], recv_sem=recv.at[n],
                device_id={"tiles": me + step}, device_id_type=MESH), there, back))
        return out

    q_copies = coarse_copies(QC, q_send, q_recv)
    p_copies = coarse_copies(PC, p_send, p_recv)
    for copy, there, _ in q_copies:
        start_all([copy], there)

    def fine_a(j, i, near):
        scale = 0.8 * land(row_tile, j)
        for t in range(4):
            k8 = 8.0 * KL[j + 1, t]
            dg = 1.0 + k8 * near[t]
            r = scale / dg
            DG[j, t] = dg
            CL[j + 1, t] = tile_of(BN, j, t) * r
            WL[j, t] = k8 * r

    local_stage(lambda n: [KL[n, t] for t in range(4)], lambda n, t: KH[n, t], fine_a)

    recv_all(b_next, has_prev)
    recv_all(b_prev, has_next)

    def halo_a(j, i, near):
        scale = jnp.where(
            side0,
            jnp.where(half0, land(prev_tile, j), land(prev_tile, j + 32)),
            jnp.where(half0, land(next_tile, j), land(next_tile, j + 32)),
        ) * 0.8
        for t in range(4):
            k8 = 8.0 * KH[j + 1, t]
            r = scale / (1.0 + k8 * near[t])
            CH[j + 1, t] = tile_of(BHN, j, t) * r
            WH[j, t] = k8 * r

    halo_stage(lambda n: [KH[n, t] for t in range(4)], lambda n, t: KL[n, t], halo_a)
    pad_halo(CH)

    MS[1] = mass_total(0)
    mass_start(1)

    def fine_b(j, i, near):
        for t in range(4):
            FL[j + 1, t] = 1.2 * CL[j + 1, t] + WL[j, t] * near[t]

    def halo_b(j, i, near):
        for t in range(4):
            FH[j + 1, t] = 1.2 * CH[j + 1, t] + WH[j, t] * near[t]

    def product(k, f):
        return lambda n: [k[n, t] * f[n, t] for t in range(4)]

    def product1(k, f):
        return lambda n, t: k[n, t] * f[n, t]

    local_stage(product(KL, CL), product1(KH, CH), fine_b)
    halo_stage(product(KH, CH), product1(KL, CL), halo_b)
    pad_halo(FH)

    def fine_c(j, i, near):
        parts = [
            (CL[j + 1, t] - 0.8 * FL[j + 1, t] + WL[j, t] * near[t]) * DG[j, t] for t in range(4)
        ]
        RS[pl.ds(pl.multiple_of((j // 4) * 8, 8), 8), pl.ds(128 * i, 128)] = (parts[0] + parts[1]) + (parts[2] + parts[3])

    local_stage(product(KL, FL), product1(KH, FH), fine_c)
    PC[2] = exact_dot(RS[...], squeeze).reshape(16, 8, 128) * GQ[...]
    for copy, there, _ in p_copies:
        start_all([copy], there)

    MS[2] = mass_total(1)
    mass_start(2)

    for copy, _, back in q_copies + p_copies:
        recv_all([copy], back)

    for slot in range(5):
        UC[pl.ds(1, 16), slot] = PC[slot]

    def coarse_sweep(old, new, slots):
        def sa(q):
            u = {slot: old[q + 1, slot] for slot in slots}
            s = []
            for slot in slots:
                up, down = rs(u[slot], 1), rs(u[slot], -1)
                if slot - 1 in u:
                    up = jnp.where(m0, rs(u[slot - 1], -3), up)
                if slot + 1 in u:
                    down = jnp.where(m3, rs(u[slot + 1], 3), down)
                s.append(up + down)
            return s, [u[slot] + 0.5 * x for slot, x in zip(slots, s)]

        def finalize(q, i, near):
            for n, slot in enumerate(slots):
                new[q + 1, slot] = 0.2 * old[q + 1, slot] + PC[slot, q] + QC[slot, q] * near[n]

        along(0, 16, sa, finalize, begin(sa, 0), 2)

    wide = range(5)
    narrow = range(1, 4)
    coarse_sweep(UC, UP, wide)
    coarse_sweep(UP, UC, wide)
    coarse_sweep(UC, UP, wide)
    coarse_sweep(UP, UC, wide)
    coarse_sweep(UC, UP, narrow)
    coarse_sweep(UP, UC, narrow)
    coarse_sweep(UC, UP, narrow)

    own = UP[pl.ds(1, 16), 2] * ICK[pl.ds(0, 16)]
    beside = []
    for q in range(8):
        above0, below0 = UP[q + 1, 1], UP[q + 1, 3]
        above1, below1 = UP[q + 9, 1], UP[q + 9, 3]
        rows = jnp.where(
            half0,
            jnp.where(side0, rs(above0, -3), rs(below0, 1)),
            jnp.where(side0, rs(above1, -1), rs(below1, 3)),
        )
        beside.append(rows * ICK[16 + q])
    OH_up = exact_dot(own.reshape(128, 128), stretch)
    RS[...] = OH_up
    OH_side = exact_dot(jnp.concatenate(beside, axis=0), stretch)

    def add_local(q, _):
        for i in range(4):
            up = RS[pl.ds(pl.multiple_of(q * 8, 8), 8), pl.ds(128 * i, 128)]
            for t in range(4):
                FL[4 * q + i + 1, t] = FL[4 * q + i + 1, t] + up
        return 0

    lax.fori_loop(0, 16, add_local, 0)
    RS[pl.ds(0, 64), :] = OH_side

    def add_halo(q, _):
        for i in range(4):
            up = RS[pl.ds(pl.multiple_of(q * 8, 8), 8), pl.ds(128 * i, 128)]
            for t in range(4):
                FH[4 * q + i + 1, t] = FH[4 * q + i + 1, t] + up
        return 0

    lax.fori_loop(0, 8, add_halo, 0)
    pad_halo(FH)

    def fine_d(j, i, near):
        for t in range(4):
            GL[j + 1, t] = 0.2 * FL[j + 1, t] + CL[j + 1, t] + WL[j, t] * near[t]

    def halo_d(j, i, near):
        for t in (0, 3):
            GH[j + 1, t] = 0.2 * FH[j + 1, t] + CH[j + 1, t] + WH[j, t] * near[t]

    local_stage(product(KL, FL), product1(KH, FH), fine_d)
    halo_stage(product(KH, FH), product1(KL, FL), halo_d)
    for t in (0, 3):
        GH[0, t] = jnp.where(half0, 0.0, rs(GH[32, t], 2))
        GH[33, t] = jnp.where(half0, rs(GH[1, t], -2), 0.0)

    mass = jnp.sum(mass_total(2))
    cells = float(2 * 16 * 8192) * ntiles * ncls
    ratio = jnp.where(sub < 4, target_ref[0], target_ref[1]) * cells / jnp.full((8, 128), mass, F32)

    def fine_e(j, i, near):
        level = ratio * land(row_tile, j)
        for t in range(4):
            f = 0.2 * GL[j + 1, t] + CL[j + 1, t] + WL[j, t] * near[t]
            OH[j, pl.ds(t, 8, stride=4), :] = f
            OF[j, pl.ds(t, 8, stride=4), :] = tile_of(SN, j, t) * level / jnp.maximum(f, FLOOR_LEVEL)

    local_stage(product(KL, GL), product1(KH, GH), fine_e)

    outs = []
    for n, (vmem, hbm) in enumerate(((OH, heat_out), (OF, flow_out))):
        for c in range(2):
            for rt in range(2):
                outs.append(pltpu.make_async_copy(
                    vmem.at[:, pl.ds(16 * c + 8 * rt, 8), :], hbm.at[c, rt], sem_out.at[4 * n + 2 * c + rt]))
    for copy in outs:
        copy.start()

    sent_all(k_next + b_next, has_next)
    sent_all(k_prev + b_prev, has_prev)
    for copy, there, _ in q_copies + p_copies:
        sent_all([copy], there)
    for stage in range(3):
        for r in range(1, sizes[stage]):
            mass_copy(stage, r).wait_send()
    for copy in outs:
        copy.wait()


def solution(mesh):
    ntiles, ncls = mesh.shape["tiles"], mesh.shape["cls"]

    def tiles_view(x):
        return x.reshape(2, 2, 8, 64, 128).transpose(0, 1, 3, 2, 4)

    def rows_view(x):
        return x.transpose(0, 1, 3, 2, 4).reshape(2, 16, 8192)

    def on_device(scaling, source, speed, tile_mask, target):
        def body(*refs):
            kernel(ntiles, ncls, *refs)

        def vmem(*shape):
            return pltpu.VMEM(shape, F32)

        dma = pltpu.SemaphoreType.DMA
        any_space = pl.BlockSpec(memory_space=pl.ANY)
        smem = pl.BlockSpec(memory_space=pltpu.SMEM)
        heat, flow = pl.pallas_call(
            body,
            out_shape=[jax.ShapeDtypeStruct((2, 2, 64, 8, 128), F32)] * 2,
            in_specs=[smem, smem, any_space, any_space, any_space],
            out_specs=[any_space, any_space],
            scratch_shapes=[
                vmem(66, 32, 128), vmem(64, 32, 128), vmem(64, 32, 128),
                vmem(34, 32, 128), vmem(32, 32, 128),
                vmem(66, 4, 8, 128), vmem(66, 4, 8, 128), vmem(64, 4, 8, 128), vmem(64, 4, 8, 128),
                vmem(66, 4, 8, 128), vmem(66, 4, 8, 128),
                vmem(34, 4, 8, 128), vmem(34, 4, 8, 128), vmem(32, 4, 8, 128),
                vmem(34, 4, 8, 128), vmem(34, 4, 8, 128),
                vmem(128, 512),
                vmem(18, 8, 128), vmem(16, 8, 128), vmem(24, 8, 128),
                vmem(5, 16, 8, 128), vmem(5, 16, 8, 128),
                vmem(18, 5, 8, 128), vmem(18, 5, 8, 128),
                vmem(64, 32, 128), vmem(64, 32, 128),
                vmem(3, 8, 128), vmem(20, 8, 128),
                dma((12,)), dma((8,)),
                dma((8,)), dma((8,)), dma((8,)), dma((8,)),
                dma((4,)), dma((4,)), dma((4,)), dma((4,)),
                dma((20,)), dma((20,)),
            ],
            compiler_params=pltpu.CompilerParams(
                collective_id=0, has_side_effects=True, vmem_limit_bytes=48 * 2**20
            ),
        )(tile_mask, target, tiles_view(scaling), tiles_view(source), tiles_view(speed))
        return rows_view(heat), rows_view(flow)

    placed = (P("cls", "tiles", None), P("cls", "tiles", None), P("cls", "tiles", None), P(), P("cls"))
    return jax.shard_map(
        on_device,
        mesh=mesh,
        in_specs=placed,
        out_specs=(P("cls", "tiles", None), P("cls", "tiles", None)),
        check_vma=False,
    )
```

time: 450 us -> 49.7 us (0.11); the launches traced: 441 us -> 49.5 us
  starting transfers between devices: 147 us -> 0 us
  local copies, waits for them, and re-layouts: 126 us -> 6.29 us
  blocking collectives: 97.9 us -> 0 us
  other arithmetic: 61.3 us -> 0 us
  Pallas kernels: 0 us -> 42.5 us
  waiting for transfers between devices: 7.72 us -> 0 us
    ppermute x30 -> x0, starting transfers between devices: 147 us -> none  [the longest x15 114 us: with_halo(): after = lax.ppermute(leading, axis, down)]
    reshape x4 -> x0, local copies, waits for them, and re-layouts: 111 us -> none  [the longest x1 51.8 us: block_mean(): field.reshape(field.shape[0], field.shape[1] // 4, 4, field.shape[2] // 4...]
    psum x1 -> x0, blocking collectives: 97.9 us -> none  [on_device(): global_mass = lax.psum(jnp.sum(source), ('tiles', 'cls'))]
    pallas_call x0 -> x1, Pallas kernels: none -> 42.5 us  [on_device(): pl.pallas_call(body, out_shape=[jax.ShapeDtypeStruct((2, 2, 64, 8, 128),...]
    reduce_sum x3 -> x0, other arithmetic: 26.6 us -> none  [the longest x1 12.2 us: block_mean(): return jnp.mean(shaped, axis=(2, 4))]
    mul x12 -> x0, other arithmetic: 19.2 us -> none  [the longest x11 15.6 us: jacobi(): land_cells * (center + OMEGA_DAMP * (right_side - applied) / coeffs[2])]
    concatenate x15 -> x0, other arithmetic: 8.77 us -> none  [with_halo(): array = jnp.concatenate([before, array, after], axis=dim)]
    ppermute x30 -> x0, waiting for transfers between devices: 7.72 us -> none  [the longest x15 7.68 us: with_halo(): after = lax.ppermute(leading, axis, down)]
  transfers between devices with their start and end apart: 30 -> 0, of which waited for: 9 -> 0; matrix products, arithmetic and copies ran while one was open for 19% -> 0% of each run, Pallas kernels for 0% -> 0%
where the time goes in v1:
time: 49.7 us; the launch traced here: 49.5 us
  Pallas kernels  42.5 us (86%)
  local copies, waits for them, and re-layouts  6.29 us (13%)
  between operations  0.66 us (1%)
    pallas_call x1, Pallas kernels, on_device(): pl.pallas_call(body, out_shape=[jax.ShapeDtypeStruct((2, 2, 64, 8, 128),...  42.5 us
    unnamed x12, local copies, waits for them, and re-layouts  6.29 us

profile of v1, /device:TPU:33, one launch (start us, length us, event | category | flops | bytes accessed | tf_op | source)
XLA Modules:
  0.0 49.5 jit_solution(16553264099350202004)
XLA Ops:
  0.6 0.0 copy-start.3
  0.6 0.0 copy-start.4
  0.7 0.7 %copy-done.3 = s32[8,32]{1,0:T(8,128)S(1)} copy-done((s32[8,32]{1,0:T(8,128)S(1)}, s32[8,32]{1,0:T(8,128)}, u32[]{:S(2)}) %copy-start.3) | copy-done | bytes 1048
  1.3 0.0 copy-done.4
  1.3 0.0 copy-start
  1.3 1.2 %copy-done = f32[2,16,8192]{2,1,0:T(8,128)S(1)} copy-done((f32[2,16,8192]{2,1,0:T(8,128)S(1)}, f32[2,16,8192]{2,1,0:T(8,128)}, u32[]{:S(2)}) %copy-start) | copy-done | bytes 1048600
  2.5 0.0 copy-start.1
  2.5 1.2 %copy-done.1 = f32[2,16,8192]{2,1,0:T(8,128)S(1)} copy-done((f32[2,16,8192]{2,1,0:T(8,128)S(1)}, f32[2,16,8192]{2,1,0:T(8,128)}, u32[]{:S(2)}) %copy-start.1) | copy-done | bytes 1048600
  3.8 0.0 copy-start.2
  3.8 1.2 %copy-done.2 = f32[2,16,8192]{2,1,0:T(8,128)S(1)} copy-done((f32[2,16,8192]{2,1,0:T(8,128)S(1)}, f32[2,16,8192]{2,1,0:T(8,128)}, u32[]{:S(2)}) %copy-start.2) | copy-done | bytes 1048600
  5.0 42.5 %shard_map.68 = (f32[2,2,64,8,128]{4,3,2,1,0:T(8,128)S(1)}, f32[2,2,64,8,128]{4,3,2,1,0:T(8,128)S(1)}) custom-call(s32[8,32]{1,0:T(8,128)S(1)} %copy-done.3, f32[2]{0:T(128)S(1)} %copy-done.4, f32[2,2,64,8,128]{4,3,2,1,0:T(8,128)S(1)} %bitcast.17, f32[2,2,64,8,128]{4,3,2,1,0:T(8,128)S(1)} %bitcast.18, f32[2,2,64,8,128]{4,3,2,1,0:T(8,128)S(1)} %bitcast.19), custom_call_target="tpu_custom_call" | custom-call | tf_op jit(solution)/shard_map/pallas_call | solution.py:564
  47.5 1.0 %copy.9 = f32[2,16,8192]{2,1,0:T(8,128)} copy(f32[2,16,8192]{2,1,0:T(8,128)S(1)} %bitcast.16) | data formatting | bytes 2097152
  48.5 1.0 %copy.10 = f32[2,16,8192]{2,1,0:T(8,128)} copy(f32[2,16,8192]{2,1,0:T(8,128)S(1)} %bitcast.15) | data formatting | bytes 2097152
Async XLA Ops:
  0.6 0.7 %copy-start.3 = (s32[8,32]{1,0:T(8,128)S(1)}, s32[8,32]{1,0:T(8,128)}, u32[]{:S(2)}) copy-start(s32[8,32]{1,0:T(8,128)} %refs_0_.1) | copy-start | bytes 3076
  0.6 0.7 %copy-start.4 = (f32[2]{0:T(128)S(1)}, f32[2]{0:T(128)}, u32[]{:S(2)}) copy-start(f32[2]{0:T(128)} %refs_1_.1) | copy-start | bytes 28
  1.3 1.2 %copy-start = (f32[2,16,8192]{2,1,0:T(8,128)S(1)}, f32[2,16,8192]{2,1,0:T(8,128)}, u32[]{:S(2)}) copy-start(f32[2,16,8192]{2,1,0:T(8,128)} %param.5) | copy-start | bytes 3145732
  2.5 1.2 %copy-start.1 = (f32[2,16,8192]{2,1,0:T(8,128)S(1)}, f32[2,16,8192]{2,1,0:T(8,128)}, u32[]{:S(2)}) copy-start(f32[2,16,8192]{2,1,0:T(8,128)} %param.6) | copy-start | bytes 3145732
  3.8 1.2 %copy-start.2 = (f32[2,16,8192]{2,1,0:T(8,128)S(1)}, f32[2,16,8192]{2,1,0:T(8,128)}, u32[]{:S(2)}) copy-start(f32[2,16,8192]{2,1,0:T(8,128)} %param.7) | copy-start | bytes 3145732

commit v2 on v1

--- a/solution.py
+++ b/solution.py
@@ -235,7 +235,7 @@
         s = [up0 + u[1], u[0] + u[2], u[1] + u[3], u[2] + down3]
         return s, [u[t] + 0.5 * s[t] for t in range(4)]
 
-    def local_stage(u_at, edge_at, finalize, unroll=4):
+    def local_stage(u_at, edge_at, finalize, unroll=32):
         def sa_of(half):
             def sa(j):
                 u = u_at(j + 1)
@@ -254,7 +254,7 @@
         carry = along(0, 32, sa_of(0), finalize, carry, unroll)
         along(32, 32, sa_of(1), finalize, carry, unroll)
 
-    def halo_stage(u_at, local_at, finalize, unroll=4):
+    def halo_stage(u_at, local_at, finalize, unroll=32):
         def sa(j):
             u = u_at(j + 1)
             up0 = jnp.where(m3, local_at(j + 33, 3), rs(local_at(j + 1, 3), -2))
@@ -415,7 +415,7 @@
         parts = [
             (CL[j + 1, t] - 0.8 * FL[j + 1, t] + WL[j, t] * near[t]) * DG[j, t] for t in range(4)
         ]
-        RS[pl.ds(pl.multiple_of((j // 4) * 8, 8), 8), pl.ds(128 * i, 128)] = (parts[0] + parts[1]) + (parts[2] + parts[3])
+        RS[pl.ds(pl.multiple_of((j // 4) * 8, 8), 8), pl.ds(128 * (i % 4), 128)] = (parts[0] + parts[1]) + (parts[2] + parts[3])
 
     local_stage(product(KL, FL), product1(KH, FH), fine_c)
     PC[2] = exact_dot(RS[...], squeeze).reshape(16, 8, 128) * GQ[...]
@@ -448,7 +448,7 @@
             for n, slot in enumerate(slots):
                 new[q + 1, slot] = 0.2 * old[q + 1, slot] + PC[slot, q] + QC[slot, q] * near[n]
 
-        along(0, 16, sa, finalize, begin(sa, 0), 2)
+        along(0, 16, sa, finalize, begin(sa, 0), 16)
 
     wide = range(5)
     narrow = range(1, 4)

time: 49.7 us -> 38.8 us (0.78)
  Pallas kernels: 42.5 us -> 31.6 us
    pallas_call x1, Pallas kernels: 42.5 us -> 31.6 us  [on_device(): pl.pallas_call(body, out_shape=[jax.ShapeDtypeStruct((2, 2, 64, 8, 128),...]
where the time goes in v2:
time: 38.8 us; the launch traced here: 38.6 us
  Pallas kernels  31.6 us (81%)
  local copies, waits for them, and re-layouts  6.29 us (16%)
  between operations  0.66 us (2%)
    pallas_call x1, Pallas kernels, on_device(): pl.pallas_call(body, out_shape=[jax.ShapeDtypeStruct((2, 2, 64, 8, 128),...  31.6 us
    unnamed x12, local copies, waits for them, and re-layouts  6.29 us

profile of v2, /device:TPU:33, one launch (start us, length us, event | category | flops | bytes accessed | tf_op | source)
XLA Modules:
  0.0 38.6 jit_solution(3787789350275144662)
XLA Ops:
  0.6 0.0 copy-start.3
  0.6 0.0 copy-start.4
  0.7 0.7 %copy-done.3 = s32[8,32]{1,0:T(8,128)S(1)} copy-done((s32[8,32]{1,0:T(8,128)S(1)}, s32[8,32]{1,0:T(8,128)}, u32[]{:S(2)}) %copy-start.3) | copy-done | bytes 1048
  1.3 0.0 copy-done.4
  1.3 0.0 copy-start
  1.3 1.2 %copy-done = f32[2,16,8192]{2,1,0:T(8,128)S(1)} copy-done((f32[2,16,8192]{2,1,0:T(8,128)S(1)}, f32[2,16,8192]{2,1,0:T(8,128)}, u32[]{:S(2)}) %copy-start) | copy-done | bytes 1048600
  2.5 0.0 copy-start.1
  2.5 1.2 %copy-done.1 = f32[2,16,8192]{2,1,0:T(8,128)S(1)} copy-done((f32[2,16,8192]{2,1,0:T(8,128)S(1)}, f32[2,16,8192]{2,1,0:T(8,128)}, u32[]{:S(2)}) %copy-start.1) | copy-done | bytes 1048600
  3.8 0.0 copy-start.2
  3.8 1.2 %copy-done.2 = f32[2,16,8192]{2,1,0:T(8,128)S(1)} copy-done((f32[2,16,8192]{2,1,0:T(8,128)S(1)}, f32[2,16,8192]{2,1,0:T(8,128)}, u32[]{:S(2)}) %copy-start.2) | copy-done | bytes 1048600
  5.0 31.6 %shard_map.68 = (f32[2,2,64,8,128]{4,3,2,1,0:T(8,128)S(1)}, f32[2,2,64,8,128]{4,3,2,1,0:T(8,128)S(1)}) custom-call(s32[8,32]{1,0:T(8,128)S(1)} %copy-done.3, f32[2]{0:T(128)S(1)} %copy-done.4, f32[2,2,64,8,128]{4,3,2,1,0:T(8,128)S(1)} %bitcast.17, f32[2,2,64,8,128]{4,3,2,1,0:T(8,128)S(1)} %bitcast.18, f32[2,2,64,8,128]{4,3,2,1,0:T(8,128)S(1)} %bitcast.19), custom_call_target="tpu_custom_call" | custom-call | tf_op jit(solution)/shard_map/pallas_call | solution.py:564
  36.6 1.0 %copy.9 = f32[2,16,8192]{2,1,0:T(8,128)} copy(f32[2,16,8192]{2,1,0:T(8,128)S(1)} %bitcast.16) | data formatting | bytes 2097152
  37.6 1.0 %copy.10 = f32[2,16,8192]{2,1,0:T(8,128)} copy(f32[2,16,8192]{2,1,0:T(8,128)S(1)} %bitcast.15) | data formatting | bytes 2097152
Async XLA Ops:
  0.6 0.7 %copy-start.3 = (s32[8,32]{1,0:T(8,128)S(1)}, s32[8,32]{1,0:T(8,128)}, u32[]{:S(2)}) copy-start(s32[8,32]{1,0:T(8,128)} %refs_0_.1) | copy-start | bytes 3076
  0.6 0.7 %copy-start.4 = (f32[2]{0:T(128)S(1)}, f32[2]{0:T(128)}, u32[]{:S(2)}) copy-start(f32[2]{0:T(128)} %refs_1_.1) | copy-start | bytes 28
  1.3 1.2 %copy-start = (f32[2,16,8192]{2,1,0:T(8,128)S(1)}, f32[2,16,8192]{2,1,0:T(8,128)}, u32[]{:S(2)}) copy-start(f32[2,16,8192]{2,1,0:T(8,128)} %param.5) | copy-start | bytes 3145732
  2.5 1.2 %copy-start.1 = (f32[2,16,8192]{2,1,0:T(8,128)S(1)}, f32[2,16,8192]{2,1,0:T(8,128)}, u32[]{:S(2)}) copy-start(f32[2,16,8192]{2,1,0:T(8,128)} %param.6) | copy-start | bytes 3145732
  3.8 1.2 %copy-start.2 = (f32[2,16,8192]{2,1,0:T(8,128)S(1)}, f32[2,16,8192]{2,1,0:T(8,128)}, u32[]{:S(2)}) copy-start(f32[2,16,8192]{2,1,0:T(8,128)} %param.7) | copy-start | bytes 3145732

commit v3 on v2

--- a/solution.py
+++ b/solution.py
@@ -14,10 +14,10 @@
 
 def kernel(
     ntiles, ncls,
-    mask_ref, target_ref, b_in, src_in, k_in,
-    heat_out, flow_out,
-    KN, BN, SN, KHN, BHN, KL, CL, WL, DG, FL, GL, KH, CH, WH, FH, GH, RS, CK, GQ, ICK, PC, QC, UC, UP, OH, OF, MS, MR,
-    sem_in, sem_out, k_send, k_recv, b_send, b_recv, q_send, q_recv, p_send, p_recv, m_send, m_recv,
+    mask_in, target_in, b_in, src_in, k_in,
+    OH, OF,
+    KN, BN, SN, KHN, BHN, KL, CL, WL, DG, FL, GL, KH, CH, WH, FH, GH, RS, CK, GQ, ICK, PC, QC, UC, UP, MS, MR, mask_ref, target_ref,
+    sem_in, k_send, k_recv, b_send, b_recv, q_send, q_recv, p_send, p_recv, m_send, m_recv,
 ):
     me = lax.axis_index("tiles")
     cl = lax.axis_index("cls")
@@ -39,6 +39,34 @@
     def rl(x, n):
         return pltpu.roll(x, n % 128, 1)
 
+    low = me % 8
+    mid = me // 8 % 2
+    high = me // 16
+    place = 2 * mid + cl
+
+    def mass_peer(stage, r):
+        if stage == 0:
+            return {"tiles": me - low + (low + r) % 8, "cls": cl}
+        if stage == 1:
+            other = (place + r) % 4
+            return {"tiles": me + 8 * (other // 2 - mid), "cls": other % 2}
+        return {"tiles": me + 16 * ((high + r) % 8 - high), "cls": cl}
+
+    sizes = (8, 4, 8)
+    starts = (0, 8, 12)
+
+    barrier = pltpu.get_barrier_semaphore()
+
+    def greet(there):
+        pl.semaphore_signal(barrier, inc=1, device_id=there, device_id_type=MESH)
+
+    for step, there in ((-1, has_prev), (1, has_next), (-2, has_prev2), (2, has_next2)):
+        @pl.when(there)
+        def _():
+            greet({"tiles": me + step})
+    for stage in range(3):
+        for r in range(1, sizes[stage]):
+            greet(mass_peer(stage, r))
     def load_copies(hbm, vmem, base, s):
         return [
             pltpu.make_async_copy(
@@ -51,37 +79,13 @@
     k_loads = load_copies(k_in, KN, 1, 0)
     b_loads = load_copies(b_in, BN, 0, 1)
     s_loads = load_copies(src_in, SN, 0, 2)
-    for copy in k_loads + s_loads + b_loads:
+    small_loads = [
+        pltpu.make_async_copy(mask_in, mask_ref, sem_in.at[12]),
+        pltpu.make_async_copy(target_in, target_ref, sem_in.at[13]),
+    ]
+    for copy in k_loads + s_loads + small_loads + b_loads:
         copy.start()
 
-    low = me % 8
-    mid = me // 8 % 2
-    high = me // 16
-    place = 2 * mid + cl
-
-    def mass_peer(stage, r):
-        if stage == 0:
-            return {"tiles": me - low + (low + r) % 8, "cls": cl}
-        if stage == 1:
-            other = (place + r) % 4
-            return {"tiles": me + 8 * (other // 2 - mid), "cls": other % 2}
-        return {"tiles": me + 16 * ((high + r) % 8 - high), "cls": cl}
-
-    sizes = (8, 4, 8)
-    starts = (0, 8, 12)
-
-    barrier = pltpu.get_barrier_semaphore()
-
-    def greet(there):
-        pl.semaphore_signal(barrier, inc=1, device_id=there, device_id_type=MESH)
-
-    for step, there in ((-1, has_prev), (1, has_next), (-2, has_prev2), (2, has_next2)):
-        @pl.when(there)
-        def _():
-            greet({"tiles": me + step})
-    for stage in range(3):
-        for r in range(1, sizes[stage]):
-            greet(mass_peer(stage, r))
     one = jnp.int32(1)
     nil = jnp.int32(0)
     greeted = 17
@@ -186,7 +190,7 @@
             total = total + MR[starts[stage] + r]
         return total
 
-    for copy in s_loads:
+    for copy in s_loads + small_loads:
         copy.wait()
 
     def add_source(n, sums):
@@ -522,15 +526,6 @@
 
     local_stage(product(KL, GL), product1(KH, GH), fine_e)
 
-    outs = []
-    for n, (vmem, hbm) in enumerate(((OH, heat_out), (OF, flow_out))):
-        for c in range(2):
-            for rt in range(2):
-                outs.append(pltpu.make_async_copy(
-                    vmem.at[:, pl.ds(16 * c + 8 * rt, 8), :], hbm.at[c, rt], sem_out.at[4 * n + 2 * c + rt]))
-    for copy in outs:
-        copy.start()
-
     sent_all(k_next + b_next, has_next)
     sent_all(k_prev + b_prev, has_prev)
     for copy, there, _ in q_copies + p_copies:
@@ -538,7 +533,20 @@
     for stage in range(3):
         for r in range(1, sizes[stage]):
             mass_copy(stage, r).wait_send()
-    for copy in outs:
+
+
+def write_out(heat, flow, heat_out, flow_out, sem):
+    copies = [
+        pltpu.make_async_copy(
+            x.at[:, pl.ds(16 * c + 8 * rt, 8), :], out.at[c, rt], sem.at[4 * n + 2 * c + rt]
+        )
+        for n, (x, out) in enumerate(((heat, heat_out), (flow, flow_out)))
+        for c in range(2)
+        for rt in range(2)
+    ]
+    for copy in copies:
+        copy.start()
+    for copy in copies:
         copy.wait()
 
 
@@ -560,12 +568,11 @@
 
         dma = pltpu.SemaphoreType.DMA
         any_space = pl.BlockSpec(memory_space=pl.ANY)
-        smem = pl.BlockSpec(memory_space=pltpu.SMEM)
         heat, flow = pl.pallas_call(
             body,
-            out_shape=[jax.ShapeDtypeStruct((2, 2, 64, 8, 128), F32)] * 2,
-            in_specs=[smem, smem, any_space, any_space, any_space],
-            out_specs=[any_space, any_space],
+            out_shape=[pltpu.VMEM((64, 32, 128), F32)] * 2,
+            in_specs=[any_space] * 5,
+            out_specs=[pl.BlockSpec(memory_space=pltpu.VMEM)] * 2,
             scratch_shapes=[
                 vmem(66, 32, 128), vmem(64, 32, 128), vmem(64, 32, 128),
                 vmem(34, 32, 128), vmem(32, 32, 128),
@@ -577,9 +584,9 @@
                 vmem(18, 8, 128), vmem(16, 8, 128), vmem(24, 8, 128),
                 vmem(5, 16, 8, 128), vmem(5, 16, 8, 128),
                 vmem(18, 5, 8, 128), vmem(18, 5, 8, 128),
-                vmem(64, 32, 128), vmem(64, 32, 128),
                 vmem(3, 8, 128), vmem(20, 8, 128),
-                dma((12,)), dma((8,)),
+                pltpu.SMEM((8, 32), jnp.int32), pltpu.SMEM((2,), F32),
+                dma((14,)),
                 dma((8,)), dma((8,)), dma((8,)), dma((8,)),
                 dma((4,)), dma((4,)), dma((4,)), dma((4,)),
                 dma((20,)), dma((20,)),
@@ -587,7 +594,18 @@
             compiler_params=pltpu.CompilerParams(
                 collective_id=0, has_side_effects=True, vmem_limit_bytes=48 * 2**20
             ),
-        )(tile_mask, target, tiles_view(scaling), tiles_view(source), tiles_view(speed))
+        )(*(
+            pltpu.with_memory_space_constraint(x, pltpu.HBM)
+            for x in (tile_mask, target, tiles_view(scaling), tiles_view(source), tiles_view(speed))
+        ))
+        heat, flow = pl.pallas_call(
+            write_out,
+            out_shape=[jax.ShapeDtypeStruct((2, 2, 64, 8, 128), F32)] * 2,
+            in_specs=[any_space] * 2,
+            out_specs=[any_space] * 2,
+            scratch_shapes=[dma((8,))],
+            compiler_params=pltpu.CompilerParams(vmem_limit_bytes=4 * 2**20),
+        )(heat, flow)
         return rows_view(heat), rows_view(flow)
 
     placed = (P("cls", "tiles", None), P("cls", "tiles", None), P("cls", "tiles", None), P(), P("cls"))

time: 38.8 us -> 32.7 us (0.84)
  local copies, waits for them, and re-layouts: 6.29 us -> 0 us
  Pallas kernels: 31.6 us -> 32 us
    unnamed x12 -> x0, local copies, waits for them, and re-layouts: 6.29 us -> none
    pallas_call x1 -> x2, Pallas kernels: 31.6 us -> 32 us  [the longest x1 30.6 us: on_device(): pl.pallas_call(body, out_shape=[pltpu.VMEM((64, 32, 128), F32)] * 2, in_s...]
where the time goes in v3:
time: 32.7 us; the launch traced here: 32.6 us
  Pallas kernels  32 us (98%)
  between operations  0.64 us (2%)
    pallas_call x1, Pallas kernels, on_device(): pl.pallas_call(body, out_shape=[pltpu.VMEM((64, 32, 128), F32)] * 2, in_s...  30.6 us
    pallas_call x1, Pallas kernels, on_device(): pl.pallas_call(write_out, out_shape=[jax.ShapeDtypeStruct((2, 2, 64, 8, 1...  1.38 us

profile of v3, /device:TPU:33, one launch (start us, length us, event | category | flops | bytes accessed | tf_op | source)
XLA Modules:
  0.0 32.6 jit_solution(14129100793769377693)
XLA Ops:
  0.6 30.6 %shard_map.68 = (f32[64,32,128]{2,1,0:T(8,128)S(1)}, f32[64,32,128]{2,1,0:T(8,128)S(1)}) custom-call(s32[8,32]{1,0:T(8,128)} %refs_0_.1, f32[2]{0:T(128)} %refs_1_.1, f32[2,2,64,8,128]{4,3,2,1,0:T(8,128)} %bitcast.15, f32[2,2,64,8,128]{4,3,2,1,0:T(8,128)} %bitcast.16, f32[2,2,64,8,128]{4,3,2,1,0:T(8,128)} %bitcast.17), custom_call_target="tpu_custom_call" | custom-call | tf_op jit(solution)/shard_map/pallas_call | solution.py:571
  31.2 1.4 %shard_map.69 = (f32[2,2,64,8,128]{4,3,2,1,0:T(8,128)}, f32[2,2,64,8,128]{4,3,2,1,0:T(8,128)}) custom-call(f32[64,32,128]{2,1,0:T(8,128)S(1)} %get-tuple-element.6.heat, f32[64,32,128]{2,1,0:T(8,128)S(1)} %get-tuple-element.7.flow), custom_call_target="tpu_custom_call" | custom-call | tf_op jit(solution)/shard_map/pallas_call | solution.py:601

commit v4 on v3

v4 whole, which is shorter than its diff:
```python
import jax
import jax.numpy as jnp
from jax import lax
from jax.experimental import pallas as pl
from jax.experimental.pallas import tpu as pltpu
from jax.sharding import PartitionSpec as P

MESH = pl.DeviceIdType.MESH
F32 = jnp.float32
BF16 = jnp.bfloat16
FLOOR_LEVEL = 0.25
TS = 256


class View:
    def __init__(self, ref, c):
        self.ref, self.c = ref, c

    def _at(self, index):
        if index is Ellipsis:
            return (self.c,)
        return (self.c,) + (index if isinstance(index, tuple) else (index,))

    def __getitem__(self, index):
        return self.ref[self._at(index)]

    def __setitem__(self, index, value):
        self.ref[self._at(index)] = value


def kernel(
    ntiles, ncls,
    mask_in, target_in, b_in, src_in, k_in,
    OH, OF,
    KN, BN, SN, KHN, BHN, KL, CL, WL, DG, FL, GL, KH, CH, WH, FH, GH, RS, RH, CK, GQ, ICK, PC, QC, UC, UP, MS, MR,
    mask_ref, target_ref,
    sem_in, k_send, k_recv, b_send, b_recv, q_send, q_recv, p_send, p_recv, m_send, m_recv,
):
    me = lax.axis_index("tiles")
    cl = lax.axis_index("cls")
    has_prev, has_next = me > 0, me < ntiles - 1
    has_prev2, has_next2 = me > 1, me < ntiles - 2

    sub = lax.broadcasted_iota(jnp.int32, (8, 128), 0)
    lane = lax.broadcasted_iota(jnp.int32, (8, 128), 1)
    s4 = sub & 3
    m0, m3 = s4 == 0, s4 == 3
    low_half = sub < 4
    quarter_even = s4 < 2
    side0 = (sub & 1) == 0
    lane0, lane127 = lane == 0, lane == 127
    zero = jnp.zeros((8, 128), F32)

    def rs(x, n):
        return pltpu.roll(x, n % 8, 0)

    def rl(x, n):
        return pltpu.roll(x, n % 128, 1)

    low = me % 8
    mid = me // 8 % 2
    high = me // 16
    place = 2 * mid + cl

    def mass_peer(stage, r):
        if stage == 0:
            return {"tiles": me - low + (low + r) % 8, "cls": cl}
        if stage == 1:
            other = (place + r) % 4
            return {"tiles": me + 8 * (other // 2 - mid), "cls": other % 2}
        return {"tiles": me + 16 * ((high + r) % 8 - high), "cls": cl}

    sizes = (8, 4, 8)
    starts = (0, 8, 12)

    barrier = pltpu.get_barrier_semaphore()

    def greet(there):
        pl.semaphore_signal(barrier, inc=1, device_id=there, device_id_type=MESH)

    for step, there in ((-1, has_prev), (1, has_next), (-2, has_prev2), (2, has_next2)):
        @pl.when(there)
        def _():
            greet({"tiles": me + step})
    for stage in range(3):
        for r in range(1, sizes[stage]):
            greet(mass_peer(stage, r))

    def load_copies(hbm, vmem, s, c):
        return [
            pltpu.make_async_copy(
                hbm.at[c, rt, pl.ds(32 * half, 32)],
                vmem.at[c, :, pl.ds(16 * half + 8 * rt, 8), :],
                sem_in.at[s * 8 + 4 * c + 2 * half + rt],
            )
            for half in range(2)
            for rt in range(2)
        ]

    k_loads = [load_copies(k_in, KN, 0, c) for c in range(2)]
    b_loads = [load_copies(b_in, BN, 1, c) for c in range(2)]
    s_loads = load_copies(src_in, SN, 2, 0) + load_copies(src_in, SN, 2, 1)
    small_loads = [
        pltpu.make_async_copy(mask_in, mask_ref, sem_in.at[24]),
        pltpu.make_async_copy(target_in, target_ref, sem_in.at[25]),
    ]
    for copy in k_loads[0] + k_loads[1] + s_loads + small_loads + b_loads[0] + b_loads[1]:
        copy.start()

    one = jnp.int32(1)
    nil = jnp.int32(0)
    greeted = 17
    for there in (has_prev, has_next, has_prev2, has_next2):
        greeted = greeted + jnp.where(there, one, nil)
    pl.semaphore_wait(barrier, greeted)

    def halo_copies(hbm, vmem, c, send, recv):
        to_next, to_prev = [], []
        for q in range(4):
            n = 8 * c + q
            to_next.append(pltpu.make_async_remote_copy(
                src_ref=hbm.at[c, 1, pl.ds(16 * q, 16), pl.ds(4, 4), :],
                dst_ref=vmem.at[c, :, pl.ds(8 * q, 4), :],
                send_sem=send.at[n], recv_sem=recv.at[n],
                device_id={"tiles": me + 1}, device_id_type=MESH))
            to_prev.append(pltpu.make_async_remote_copy(
                src_ref=hbm.at[c, 0, pl.ds(16 * q, 16), pl.ds(0, 4), :],
                dst_ref=vmem.at[c, :, pl.ds(8 * q + 4, 4), :],
                send_sem=send.at[4 + n], recv_sem=recv.at[4 + n],
                device_id={"tiles": me - 1}, device_id_type=MESH))
        return to_next, to_prev

    def start_all(copies, there):
        @pl.when(there)
        def _():
            for copy in copies:
                copy.start()

    def recv_all(copies, there):
        @pl.when(there)
        def _():
            for copy in copies:
                copy.wait_recv()

    def sent_all(copies, there):
        @pl.when(there)
        def _():
            for copy in copies:
                copy.wait_send()

    k_halo = [halo_copies(k_in, KHN, c, k_send, k_recv) for c in range(2)]
    b_halo = [halo_copies(b_in, BHN, c, b_send, b_recv) for c in range(2)]
    for c in range(2):
        for to_next, to_prev in (k_halo[c], b_halo[c]):
            start_all(to_next, has_next)
            start_all(to_prev, has_prev)

    def outside(first, there):
        @pl.when(jnp.logical_not(there))
        def _():
            for c in range(2):
                for q in range(4):
                    KHN[c, :, pl.ds(8 * q + first, 4), :] = jnp.zeros((16, 4, 128), F32)
                    BHN[c, :, pl.ds(8 * q + first, 4), :] = jnp.zeros((16, 4, 128), F32)

    outside(0, has_prev)
    outside(4, has_next)

    def clear(slot, there):
        @pl.when(jnp.logical_not(there))
        def _():
            for c in range(2):
                PC[c, slot] = jnp.zeros((8, 8, 128), F32)
                QC[c, slot] = jnp.zeros((8, 8, 128), F32)

    clear(0, has_prev2)
    clear(1, has_prev)
    clear(3, has_next)
    clear(4, has_next2)

    def mass_copy(stage, r):
        return pltpu.make_async_remote_copy(
            src_ref=MS.at[stage], dst_ref=MR.at[starts[stage] + r],
            send_sem=m_send.at[starts[stage] + r], recv_sem=m_recv.at[starts[stage] + r],
            device_id=mass_peer(stage, r), device_id_type=MESH)

    def mass_start(stage):
        for r in range(1, sizes[stage]):
            mass_copy(stage, r).start()

    def mass_total(stage):
        total = MS[stage]
        for r in range(1, sizes[stage]):
            mass_copy(stage, r).wait_recv()
        for r in range(1, sizes[stage]):
            total = total + MR[starts[stage] + r]
        return total

    for copy in s_loads + small_loads:
        copy.wait()

    def add_source(n, sums):
        return tuple(
            sums[i] + SN[i // 4, n, pl.ds(8 * (i % 4), 8), :] for i in range(8)
        )

    sums = lax.fori_loop(0, 32, add_source, (zero,) * 8)
    total = sums[0]
    for part in sums[1:]:
        total = total + part
    MS[0] = total
    mass_start(0)

    row_tile = me * 16 // TS
    prev_tile = jnp.maximum(me * 16 - 1, 0) // TS
    next_tile = jnp.minimum(me * 16 + 16, ntiles * 16 - 1) // TS

    def land(row, block):
        return mask_ref[row, block // 2].astype(F32)

    def land_local(j):
        return jnp.where(low_half, land(row_tile, j), land(row_tile, j + 32))

    def land_halo(j):
        def pick(row):
            return jnp.where(
                low_half,
                jnp.where(quarter_even, land(row, j), land(row, j + 16)),
                jnp.where(quarter_even, land(row, j + 32), land(row, j + 48)),
            )
        return jnp.where(side0, pick(prev_tile), pick(next_tile))

    def along(first, count, sa, finalize, carry):
        def body(n, carry):
            for i in range(count):
                j = first + n + i
                before, s, right, left = carry
                s_next, a_next = sa(j + 1)
                right_next = [rl(x, 1) for x in a_next]
                left_next = [rl(x, -1) for x in a_next]
                near = [
                    s[t] + jnp.where(lane0, before[t], right[t]) + jnp.where(lane127, left_next[t], left[t])
                    for t in range(len(s))
                ]
                finalize(j, i, near)
                carry = (right, s_next, right_next, left_next)
            return carry

        return lax.fori_loop(0, 1, body, carry)

    def begin(sa, first):
        _, a_before = sa(first - 1)
        s, a = sa(first)
        return ([rl(x, 1) for x in a_before], s, [rl(x, 1) for x in a], [rl(x, -1) for x in a])

    def sums_of(u, up0, down3):
        s = [up0 + u[1], u[0] + u[2], u[1] + u[3], u[2] + down3]
        return s, [u[t] + 0.5 * s[t] for t in range(4)]

    def local_stage(u_at, edge_at, finalize):
        def sa_of(odd):
            def sa(j):
                u = u_at(j + 1)
                h = j - 16 * odd + 1
                above, below = edge_at(h, 3), edge_at(h, 0)
                if odd:
                    above = rs(above, -2)
                else:
                    below = rs(below, 2)
                return sums_of(
                    u, jnp.where(m0, above, rs(u[3], 1)), jnp.where(m3, below, rs(u[0], -1))
                )
            return sa

        carry = begin(sa_of(0), 0)
        carry = along(0, 16, sa_of(0), finalize, carry)
        along(16, 16, sa_of(1), finalize, carry)

    def halo_stage(u_at, local_at, finalize):
        def sa(j):
            u = u_at(j + 1)
            up0 = jnp.where(m3, local_at(j + 17, 3), rs(local_at(j + 1, 3), -2))
            down3 = jnp.where(m0, local_at(j + 1, 0), rs(local_at(j + 17, 0), 2))
            return sums_of(u, up0, down3)

        along(0, 16, sa, finalize, begin(sa, 0))

    def pad_local(ref):
        for t in range(4):
            ref[0, t] = jnp.where(low_half, 0.0, rs(ref[32, t], 4))
            ref[33, t] = jnp.where(low_half, rs(ref[1, t], 4), 0.0)

    def pad_halo(ref, tiles=(0, 1, 2, 3)):
        for t in tiles:
            ref[0, t] = jnp.where(sub < 2, 0.0, rs(ref[16, t], 2))
            ref[17, t] = jnp.where(sub < 6, rs(ref[1, t], -2), 0.0)

    def tile_of(ref, n, t):
        return ref[n, pl.ds(t, 8, stride=4), :]

    fine_lane = lax.broadcasted_iota(jnp.int32, (512, 128), 0)
    coarse_lane = lax.broadcasted_iota(jnp.int32, (512, 128), 1)
    squeeze = jnp.where(fine_lane // 4 == coarse_lane, 1.0, 0.0).astype(BF16)
    fine_lane2 = lax.broadcasted_iota(jnp.int32, (128, 512), 1)
    coarse_lane2 = lax.broadcasted_iota(jnp.int32, (128, 512), 0)
    stretch = jnp.where(fine_lane2 // 4 == coarse_lane2, 1.0, 0.0).astype(BF16)

    def exact_dot(x, y):
        high_part = x.astype(BF16)
        rest = x - high_part.astype(F32)
        middle = rest.astype(BF16)
        low_part = (rest - middle.astype(F32)).astype(BF16)
        out = jnp.dot(high_part, y, preferred_element_type=F32)
        out = out + jnp.dot(middle, y, preferred_element_type=F32)
        return out + jnp.dot(low_part, y, preferred_element_type=F32)

    def product(k, f):
        return lambda n: [k[n, t] * f[n, t] for t in range(4)]

    def product1(k, f):
        return lambda n, t: k[n, t] * f[n, t]

    def band_speed(c):
        for copy in k_loads[c]:
            copy.wait()
        kn, kl, rsum = View(KN, c), View(KL, c), View(RS, c)

        def body(q, _):
            for i in range(4):
                tiles = [tile_of(kn, 4 * q + i, t) for t in range(4)]
                for t in range(4):
                    kl[4 * q + i + 1, t] = tiles[t]
                rsum[pl.ds(pl.multiple_of(q * 8, 8), 8), pl.ds(128 * i, 128)] = (tiles[0] + tiles[1]) + (tiles[2] + tiles[3])
            return 0

        lax.fori_loop(0, 8, body, 0)
        pad_local(kl)
        CK[c] = (exact_dot(rsum[...], squeeze) * 0.0625).reshape(8, 8, 128)

    def coarse_copies(ref, c, send, recv):
        out = []
        for n, (step, there, back) in enumerate(
            ((1, has_next, has_prev), (-1, has_prev, has_next), (2, has_next2, has_prev2), (-2, has_prev2, has_next2))
        ):
            out.append((pltpu.make_async_remote_copy(
                src_ref=ref.at[c, 2], dst_ref=ref.at[c, 2 - step],
                send_sem=send.at[4 * c + n], recv_sem=recv.at[4 * c + n],
                device_id={"tiles": me + step}, device_id_type=MESH), there, back))
        return out

    q_copies = [coarse_copies(QC, c, q_send, q_recv) for c in range(2)]
    p_copies = [coarse_copies(PC, c, p_send, p_recv) for c in range(2)]

    def down(c):
        kl, cl_, wl, dgr, fl = View(KL, c), View(CL, c), View(WL, c), View(DG, c), View(FL, c)
        kh, ch, wh, fh = View(KH, c), View(CH, c), View(WH, c), View(FH, c)
        khn, bn, bhn, rsum = View(KHN, c), View(BN, c), View(BHN, c), View(RS, c)

        recv_all(k_halo[c][0], has_prev)
        recv_all(k_halo[c][1], has_next)

        def halo_speed(q, _):
            for i in range(4):
                tiles = [tile_of(khn, 4 * q + i, t) for t in range(4)]
                for t in range(4):
                    kh[4 * q + i + 1, t] = tiles[t]
                rsum[pl.ds(pl.multiple_of(q * 8, 8), 8), pl.ds(128 * i, 128)] = (tiles[0] + tiles[1]) + (tiles[2] + tiles[3])
            return 0

        lax.fori_loop(0, 4, halo_speed, 0)
        pad_halo(kh)
        ckh = (exact_dot(rsum[pl.ds(0, 32), :], squeeze) * 0.0625).reshape(4, 8, 128)

        def coarse_sa(q):
            ck = CK[c, q]
            h = ckh[q % 4]
            if q < 4:
                above, below = h, rs(h, 2)
            else:
                above, below = rs(h, -2), h
            s = jnp.where(m0, above, rs(ck, 1)) + jnp.where(m3, below, rs(ck, -1))
            return s, ck + 0.5 * s

        pairs = [coarse_sa(q) for q in range(8)]
        right = [rl(a, 1) for _, a in pairs]
        left = [rl(a, -1) for _, a in pairs]
        right_pad = jnp.where(low_half, 0.0, rs(right[7], 4))
        left_pad = jnp.where(low_half, rs(left[0], 4), 0.0)
        for q in range(8):
            ck = CK[c, q]
            near = (
                pairs[q][0]
                + jnp.where(lane0, right[q - 1] if q else right_pad, right[q])
                + jnp.where(lane127, left[q + 1] if q < 7 else left_pad, left[q])
            )
            land_q = jnp.where(lane < 64, land_local(4 * q), land_local(4 * q + 2))
            g = ck * land_q / (16.0 + 32.0 * ck * near)
            GQ[c, q] = g
            QC[c, 2, q] = 25.6 * ck * g
            ICK[c, q] = 1.0 / ck
        for q in range(4):
            ICK[c, 8 + q] = 1.0 / jnp.maximum(ckh[q], 1e-30)
        for copy, there, _ in q_copies[c]:
            start_all([copy], there)

        for copy in b_loads[c]:
            copy.wait()

        def fine_a(j, i, near):
            scale = 0.8 * land_local(j)
            for t in range(4):
                k8 = 8.0 * kl[j + 1, t]
                dg = 1.0 + k8 * near[t]
                r = scale / dg
                dgr[j, t] = dg
                cl_[j + 1, t] = tile_of(bn, j, t) * r
                wl[j, t] = k8 * r

        local_stage(lambda n: [kl[n, t] for t in range(4)], lambda n, t: kh[n, t], fine_a)
        pad_local(cl_)

        recv_all(b_halo[c][0], has_prev)
        recv_all(b_halo[c][1], has_next)

        def halo_a(j, i, near):
            scale = 0.8 * land_halo(j)
            for t in range(4):
                k8 = 8.0 * kh[j + 1, t]
                r = scale / (1.0 + k8 * near[t])
                ch[j + 1, t] = tile_of(bhn, j, t) * r
                wh[j, t] = k8 * r

        halo_stage(lambda n: [kh[n, t] for t in range(4)], lambda n, t: kl[n, t], halo_a)
        pad_halo(ch)

        def fine_b(j, i, near):
            for t in range(4):
                fl[j + 1, t] = 1.2 * cl_[j + 1, t] + wl[j, t] * near[t]

        def halo_b(j, i, near):
            for t in range(4):
                fh[j + 1, t] = 1.2 * ch[j + 1, t] + wh[j, t] * near[t]

        local_stage(product(kl, cl_), product1(kh, ch), fine_b)
        halo_stage(product(kh, ch), product1(kl, cl_), halo_b)
        pad_local(fl)
        pad_halo(fh)

        def fine_c(j, i, near):
            parts = [
                (cl_[j + 1, t] - 0.8 * fl[j + 1, t] + wl[j, t] * near[t]) * dgr[j, t] for t in range(4)
            ]
            rsum[pl.ds(pl.multiple_of((j // 4) * 8, 8), 8), pl.ds(128 * (i % 4), 128)] = (parts[0] + parts[1]) + (parts[2] + parts[3])

        local_stage(product(kl, fl), product1(kh, fh), fine_c)
        PC[c, 2] = exact_dot(rsum[...], squeeze).reshape(8, 8, 128) * GQ[c]
        for copy, there, _ in p_copies[c]:
            start_all([copy], there)

    def coarse_sweep(c, old, new, slots):
        def sa(q):
            u = {slot: old[q + 1, slot] for slot in slots}
            s = []
            for slot in slots:
                up, dn = rs(u[slot], 1), rs(u[slot], -1)
                if slot - 1 in u:
                    up = jnp.where(m0, rs(u[slot - 1], -3), up)
                if slot + 1 in u:
                    dn = jnp.where(m3, rs(u[slot + 1], 3), dn)
                s.append(up + dn)
            return s, [u[slot] + 0.5 * x for slot, x in zip(slots, s)]

        def finalize(q, i, near):
            for n, slot in enumerate(slots):
                new[q + 1, slot] = 0.2 * old[q + 1, slot] + PC[c, slot, q] + QC[c, slot, q] * near[n]

        along(0, 8, sa, finalize, begin(sa, 0))
        coarse_pads(new, slots)

    def coarse_pads(ref, slots):
        for slot in slots:
            ref[0, slot] = jnp.where(low_half, 0.0, rs(ref[8, slot], 4))
            ref[9, slot] = jnp.where(low_half, rs(ref[1, slot], 4), 0.0)

    wide = range(5)
    narrow = range(1, 4)

    def up(c):
        kl, cl_, wl, fl, gl = View(KL, c), View(CL, c), View(WL, c), View(FL, c), View(GL, c)
        kh, ch, wh, fh, gh = View(KH, c), View(CH, c), View(WH, c), View(FH, c), View(GH, c)
        uc, uq, rsum, rhal = View(UC, c), View(UP, c), View(RS, c), View(RH, c)
        for copy, _, back in q_copies[c] + p_copies[c]:
            recv_all([copy], back)
        for slot in range(5):
            uc[pl.ds(1, 8), slot] = PC[c, slot]
        coarse_pads(uc, wide)

        def two_sweeps(n, _):
            coarse_sweep(c, uc, uq, wide)
            coarse_sweep(c, uq, uc, wide)
            return 0

        lax.fori_loop(0, 2, two_sweeps, 0)
        coarse_sweep(c, uc, uq, narrow)
        coarse_sweep(c, uq, uc, narrow)
        coarse_sweep(c, uc, uq, narrow)

        own = uq[pl.ds(1, 8), 2] * ICK[c, pl.ds(0, 8)]
        beside = []
        for q in range(4):
            above0, below0 = uq[q + 1, 1], uq[q + 1, 3]
            above1, below1 = uq[q + 5, 1], uq[q + 5, 3]
            rows = jnp.where(
                quarter_even,
                jnp.where(side0, rs(above0, -3), rs(below0, 1)),
                jnp.where(side0, rs(above1, -1), rs(below1, 3)),
            )
            beside.append(rows * ICK[c, 8 + q])
        rsum[...] = exact_dot(own.reshape(64, 128), stretch)
        rhal[...] = exact_dot(jnp.concatenate(beside, axis=0), stretch)

        def add_up(count, field, part):
            def body(q, _):
                for i in range(4):
                    more = part[pl.ds(pl.multiple_of(q * 8, 8), 8), pl.ds(128 * i, 128)]
                    for t in range(4):
                        field[4 * q + i + 1, t] = field[4 * q + i + 1, t] + more
                return 0

            lax.fori_loop(0, count, body, 0)

        add_up(8, fl, rsum)
        add_up(4, fh, rhal)
        pad_local(fl)
        pad_halo(fh)

        def fine_d(j, i, near):
            for t in range(4):
                gl[j + 1, t] = 0.2 * fl[j + 1, t] + cl_[j + 1, t] + wl[j, t] * near[t]

        def halo_d(j, i, near):
            for t in (0, 3):
                gh[j + 1, t] = 0.2 * fh[j + 1, t] + ch[j + 1, t] + wh[j, t] * near[t]

        local_stage(product(kl, fl), product1(kh, fh), fine_d)
        halo_stage(product(kh, fh), product1(kl, fl), halo_d)
        pad_local(gl)
        pad_halo(gh, (0, 3))

    def last(c, mass):
        kl, cl_, wl, gl = View(KL, c), View(CL, c), View(WL, c), View(GL, c)
        kh, gh, sn, oh, of = View(KH, c), View(GH, c), View(SN, c), View(OH, c), View(OF, c)
        cells = float(2 * 16 * 8192) * ntiles * ncls
        ratio = jnp.full((8, 128), target_ref[c] * cells, F32) / mass

        def fine_e(j, i, near):
            level = ratio * land_local(j)
            for t in range(4):
                f = 0.2 * gl[j + 1, t] + cl_[j + 1, t] + wl[j, t] * near[t]
                oh[j, pl.ds(t, 8, stride=4), :] = f
                of[j, pl.ds(t, 8, stride=4), :] = tile_of(sn, j, t) * level / jnp.maximum(f, FLOOR_LEVEL)

        local_stage(product(kl, gl), product1(kh, gh), fine_e)

    band_speed(0)
    band_speed(1)
    down(0)
    MS[1] = mass_total(0)
    mass_start(1)
    down(1)
    MS[2] = mass_total(1)
    mass_start(2)
    up(0)
    up(1)
    mass = jnp.full((8, 128), jnp.sum(mass_total(2)), F32)
    last(0, mass)
    last(1, mass)

    for c in range(2):
        sent_all(k_halo[c][0] + b_halo[c][0], has_next)
        sent_all(k_halo[c][1] + b_halo[c][1], has_prev)
        for copy, there, _ in q_copies[c] + p_copies[c]:
            sent_all([copy], there)
    for stage in range(3):
        for r in range(1, sizes[stage]):
            mass_copy(stage, r).wait_send()


def write_out(heat, flow, heat_out, flow_out, sem):
    copies = [
        pltpu.make_async_copy(
            x.at[c, :, pl.ds(16 * half + 8 * rt, 8), :],
            out.at[c, rt, pl.ds(32 * half, 32)],
            sem.at[8 * n + 4 * c + 2 * half + rt],
        )
        for n, (x, out) in enumerate(((heat, heat_out), (flow, flow_out)))
        for c in range(2)
        for half in range(2)
        for rt in range(2)
    ]
    for copy in copies:
        copy.start()
    for copy in copies:
        copy.wait()


def solution(mesh):
    ntiles, ncls = mesh.shape["tiles"], mesh.shape["cls"]

    def tiles_view(x):
        return x.reshape(2, 2, 8, 64, 128).transpose(0, 1, 3, 2, 4)

    def rows_view(x):
        return x.transpose(0, 1, 3, 2, 4).reshape(2, 16, 8192)

    def on_device(scaling, source, speed, tile_mask, target):
        def body(*refs):
            kernel(ntiles, ncls, *refs)

        def vmem(*shape):
            return pltpu.VMEM(shape, F32)

        dma = pltpu.SemaphoreType.DMA
        any_space = pl.BlockSpec(memory_space=pl.ANY)
        heat, flow = pl.pallas_call(
            body,
            out_shape=[pltpu.VMEM((2, 32, 32, 128), F32)] * 2,
            in_specs=[any_space] * 5,
            out_specs=[pl.BlockSpec(memory_space=pltpu.VMEM)] * 2,
            scratch_shapes=[
                vmem(2, 32, 32, 128), vmem(2, 32, 32, 128), vmem(2, 32, 32, 128),
                vmem(2, 16, 32, 128), vmem(2, 16, 32, 128),
                vmem(2, 34, 4, 8, 128), vmem(2, 34, 4, 8, 128),
                vmem(2, 32, 4, 8, 128), vmem(2, 32, 4, 8, 128),
                vmem(2, 34, 4, 8, 128), vmem(2, 34, 4, 8, 128),
                vmem(2, 18, 4, 8, 128), vmem(2, 18, 4, 8, 128), vmem(2, 16, 4, 8, 128),
                vmem(2, 18, 4, 8, 128), vmem(2, 18, 4, 8, 128),
                vmem(2, 64, 512), vmem(2, 32, 512),
                vmem(2, 8, 8, 128), vmem(2, 8, 8, 128), vmem(2, 12, 8, 128),
                vmem(2, 5, 8, 8, 128), vmem(2, 5, 8, 8, 128),
                vmem(2, 10, 5, 8, 128), vmem(2, 10, 5, 8, 128),
                vmem(3, 8, 128), vmem(20, 8, 128),
                pltpu.SMEM((8, 32), jnp.int32), pltpu.SMEM((2,), F32),
                dma((26,)),
                dma((16,)), dma((16,)), dma((16,)), dma((16,)),
                dma((8,)), dma((8,)), dma((8,)), dma((8,)),
                dma((20,)), dma((20,)),
            ],
            compiler_params=pltpu.CompilerParams(
                collective_id=0, has_side_effects=True, vmem_limit_bytes=48 * 2**20
            ),
        )(*(
            pltpu.with_memory_space_constraint(x, pltpu.HBM)
            for x in (tile_mask, target, tiles_view(scaling), tiles_view(source), tiles_view(speed))
        ))
        heat, flow = pl.pallas_call(
            write_out,
            out_shape=[jax.ShapeDtypeStruct((2, 2, 64, 8, 128), F32)] * 2,
            in_specs=[any_space] * 2,
            out_specs=[any_space] * 2,
            scratch_shapes=[dma((16,))],
            compiler_params=pltpu.CompilerParams(vmem_limit_bytes=4 * 2**20),
        )(heat, flow)
        return rows_view(heat), rows_view(flow)

    placed = (P("cls", "tiles", None), P("cls", "tiles", None), P("cls", "tiles", None), P(), P("cls"))
    return jax.shard_map(
        on_device,
        mesh=mesh,
        in_specs=placed,
        out_specs=(P("cls", "tiles", None), P("cls", "tiles", None)),
        check_vma=False,
    )
```

time: 32.7 us -> 32.2 us (0.985)
  Pallas kernels: 32 us -> 31.3 us
    pallas_call x1, Pallas kernels: 30.6 us -> 29.9 us  [on_device(): pl.pallas_call(body, out_shape=[pltpu.VMEM((2, 32, 32, 128), F32)] * 2, i...]
where the time goes in v4:
time: 32.2 us; the launch traced here: 31.9 us
  Pallas kernels  31.3 us (97%)
  between operations  0.64 us (2%)
    pallas_call x1, Pallas kernels, on_device(): pl.pallas_call(body, out_shape=[pltpu.VMEM((2, 32, 32, 128), F32)] * 2, i...  29.9 us
    pallas_call x1, Pallas kernels, on_device(): pl.pallas_call(write_out, out_shape=[jax.ShapeDtypeStruct((2, 2, 64, 8, 1...  1.44 us

profile of v4, /device:TPU:33, one launch (start us, length us, event | category | flops | bytes accessed | tf_op | source)
XLA Modules:
  0.0 31.9 jit_solution(6872730739791802819)
XLA Ops:
  0.6 29.9 %shard_map.68 = (f32[2,32,32,128]{3,2,1,0:T(8,128)S(1)}, f32[2,32,32,128]{3,2,1,0:T(8,128)S(1)}) custom-call(s32[8,32]{1,0:T(8,128)} %refs_0_.1, f32[2]{0:T(128)} %refs_1_.1, f32[2,2,64,8,128]{4,3,2,1,0:T(8,128)} %bitcast.15, f32[2,2,64,8,128]{4,3,2,1,0:T(8,128)} %bitcast.16, f32[2,2,64,8,128]{4,3,2,1,0:T(8,128)} %bitcast.17), custom_call_target="tpu_custom_call" | custom-call | tf_op jit(solution)/shard_map/pallas_call | solution.py:625
  30.5 1.4 %shard_map.69 = (f32[2,2,64,8,128]{4,3,2,1,0:T(8,128)}, f32[2,2,64,8,128]{4,3,2,1,0:T(8,128)}) custom-call(f32[2,32,32,128]{3,2,1,0:T(8,128)S(1)} %get-tuple-element.6.heat, f32[2,32,32,128]{3,2,1,0:T(8,128)S(1)} %get-tuple-element.7.flow), custom_call_target="tpu_custom_call" | custom-call | tf_op jit(solution)/shard_map/pallas_call | solution.py:656

commit v5 on v4

--- a/solution.py
+++ b/solution.py
@@ -28,19 +28,7 @@
         self.ref[self._at(index)] = value
 
 
-def kernel(
-    ntiles, ncls,
-    mask_in, target_in, b_in, src_in, k_in,
-    OH, OF,
-    KN, BN, SN, KHN, BHN, KL, CL, WL, DG, FL, GL, KH, CH, WH, FH, GH, RS, RH, CK, GQ, ICK, PC, QC, UC, UP, MS, MR,
-    mask_ref, target_ref,
-    sem_in, k_send, k_recv, b_send, b_recv, q_send, q_recv, p_send, p_recv, m_send, m_recv,
-):
-    me = lax.axis_index("tiles")
-    cl = lax.axis_index("cls")
-    has_prev, has_next = me > 0, me < ntiles - 1
-    has_prev2, has_next2 = me > 1, me < ntiles - 2
-
+def stencil():
     sub = lax.broadcasted_iota(jnp.int32, (8, 128), 0)
     lane = lax.broadcasted_iota(jnp.int32, (8, 128), 1)
     s4 = sub & 3
@@ -56,6 +44,104 @@
 
     def rl(x, n):
         return pltpu.roll(x, n % 128, 1)
+
+    def along(first, count, sa, finalize, carry):
+        def body(n, carry):
+            for i in range(count):
+                j = first + n + i
+                before, s, right, left = carry
+                s_next, a_next = sa(j + 1)
+                right_next = [rl(x, 1) for x in a_next]
+                left_next = [rl(x, -1) for x in a_next]
+                near = [
+                    s[t] + jnp.where(lane0, before[t], right[t]) + jnp.where(lane127, left_next[t], left[t])
+                    for t in range(len(s))
+                ]
+                finalize(j, i, near)
+                carry = (right, s_next, right_next, left_next)
+            return carry
+
+        return lax.fori_loop(0, 1, body, carry)
+
+    def begin(sa, first):
+        _, a_before = sa(first - 1)
+        s, a = sa(first)
+        return ([rl(x, 1) for x in a_before], s, [rl(x, 1) for x in a], [rl(x, -1) for x in a])
+
+    def sums_of(u, up0, down3):
+        s = [up0 + u[1], u[0] + u[2], u[1] + u[3], u[2] + down3]
+        return s, [u[t] + 0.5 * s[t] for t in range(4)]
+
+    def local_stage(u_at, edge_at, finalize):
+        def sa_of(odd):
+            def sa(j):
+                u = u_at(j + 1)
+                h = j - 16 * odd + 1
+                above, below = edge_at(h, 3), edge_at(h, 0)
+                if odd:
+                    above = rs(above, -2)
+                else:
+                    below = rs(below, 2)
+                return sums_of(
+                    u, jnp.where(m0, above, rs(u[3], 1)), jnp.where(m3, below, rs(u[0], -1))
+                )
+            return sa
+
+        carry = begin(sa_of(0), 0)
+        carry = along(0, 16, sa_of(0), finalize, carry)
+        along(16, 16, sa_of(1), finalize, carry)
+
+    def halo_stage(u_at, local_at, finalize):
+        def sa(j):
+            u = u_at(j + 1)
+            up0 = jnp.where(m3, local_at(j + 17, 3), rs(local_at(j + 1, 3), -2))
+            down3 = jnp.where(m0, local_at(j + 1, 0), rs(local_at(j + 17, 0), 2))
+            return sums_of(u, up0, down3)
+
+        along(0, 16, sa, finalize, begin(sa, 0))
+
+    def pad_local(ref):
+        for t in range(4):
+            ref[0, t] = jnp.where(low_half, 0.0, rs(ref[32, t], 4))
+            ref[33, t] = jnp.where(low_half, rs(ref[1, t], 4), 0.0)
+
+    def pad_halo(ref, tiles=(0, 1, 2, 3)):
+        for t in tiles:
+            ref[0, t] = jnp.where(sub < 2, 0.0, rs(ref[16, t], 2))
+            ref[17, t] = jnp.where(sub < 6, rs(ref[1, t], -2), 0.0)
+
+    def tile_of(ref, n, t):
+        return ref[n, pl.ds(t, 8, stride=4), :]
+
+    def product(k, f):
+        return lambda n: [k[n, t] * f[n, t] for t in range(4)]
+
+    def product1(k, f):
+        return lambda n, t: k[n, t] * f[n, t]
+
+    return (
+        sub, lane, s4, m0, m3, low_half, quarter_even, side0, lane0, lane127, zero, rs,
+        rl, local_stage, halo_stage, pad_local, pad_halo, tile_of, product, product1,
+    )
+
+
+def kernel(
+    ntiles, ncls,
+    mask_in, target_in, b_in, src_in, k_in,
+    KL, CL, WL, GL, KH, GH, SN, LV,
+    KN, BN, KHN, BHN, DG, FL, CH, WH, FH, RS, RH, CK, GQ, ICK, PC, QC, MS, MR,
+    mask_ref, target_ref,
+    sem_in, k_send, k_recv, b_send, b_recv, q_send, q_recv, p_send, p_recv, m_send, m_recv,
+):
+    me = lax.axis_index("tiles")
+    cl = lax.axis_index("cls")
+    has_prev, has_next = me > 0, me < ntiles - 1
+    has_prev2, has_next2 = me > 1, me < ntiles - 2
+
+    (
+        sub, lane, s4, m0, m3, low_half, quarter_even, side0, lane0, lane127, zero, rs,
+        rl, local_stage, halo_stage, pad_local, pad_halo, tile_of, product, product1,
+    ) = stencil()
 
     low = me % 8
     mid = me // 8 % 2
@@ -230,74 +316,6 @@
             )
         return jnp.where(side0, pick(prev_tile), pick(next_tile))
 
-    def along(first, count, sa, finalize, carry):
-        def body(n, carry):
-            for i in range(count):
-                j = first + n + i
-                before, s, right, left = carry
-                s_next, a_next = sa(j + 1)
-                right_next = [rl(x, 1) for x in a_next]
-                left_next = [rl(x, -1) for x in a_next]
-                near = [
-                    s[t] + jnp.where(lane0, before[t], right[t]) + jnp.where(lane127, left_next[t], left[t])
-                    for t in range(len(s))
-                ]
-                finalize(j, i, near)
-                carry = (right, s_next, right_next, left_next)
-            return carry
-
-        return lax.fori_loop(0, 1, body, carry)
-
-    def begin(sa, first):
-        _, a_before = sa(first - 1)
-        s, a = sa(first)
-        return ([rl(x, 1) for x in a_before], s, [rl(x, 1) for x in a], [rl(x, -1) for x in a])
-
-    def sums_of(u, up0, down3):
-        s = [up0 + u[1], u[0] + u[2], u[1] + u[3], u[2] + down3]
-        return s, [u[t] + 0.5 * s[t] for t in range(4)]
-
-    def local_stage(u_at, edge_at, finalize):
-        def sa_of(odd):
-            def sa(j):
-                u = u_at(j + 1)
-                h = j - 16 * odd + 1
-                above, below = edge_at(h, 3), edge_at(h, 0)
-                if odd:
-                    above = rs(above, -2)
-                else:
-                    below = rs(below, 2)
-                return sums_of(
-                    u, jnp.where(m0, above, rs(u[3], 1)), jnp.where(m3, below, rs(u[0], -1))
-                )
-            return sa
-
-        carry = begin(sa_of(0), 0)
-        carry = along(0, 16, sa_of(0), finalize, carry)
-        along(16, 16, sa_of(1), finalize, carry)
-
-    def halo_stage(u_at, local_at, finalize):
-        def sa(j):
-            u = u_at(j + 1)
-            up0 = jnp.where(m3, local_at(j + 17, 3), rs(local_at(j + 1, 3), -2))
-            down3 = jnp.where(m0, local_at(j + 1, 0), rs(local_at(j + 17, 0), 2))
-            return sums_of(u, up0, down3)
-
-        along(0, 16, sa, finalize, begin(sa, 0))
-
-    def pad_local(ref):
-        for t in range(4):
-            ref[0, t] = jnp.where(low_half, 0.0, rs(ref[32, t], 4))
-            ref[33, t] = jnp.where(low_half, rs(ref[1, t], 4), 0.0)
-
-    def pad_halo(ref, tiles=(0, 1, 2, 3)):
-        for t in tiles:
-            ref[0, t] = jnp.where(sub < 2, 0.0, rs(ref[16, t], 2))
-            ref[17, t] = jnp.where(sub < 6, rs(ref[1, t], -2), 0.0)
-
-    def tile_of(ref, n, t):
-        return ref[n, pl.ds(t, 8, stride=4), :]
-
     fine_lane = lax.broadcasted_iota(jnp.int32, (512, 128), 0)
     coarse_lane = lax.broadcasted_iota(jnp.int32, (512, 128), 1)
     squeeze = jnp.where(fine_lane // 4 == coarse_lane, 1.0, 0.0).astype(BF16)
@@ -313,12 +331,6 @@
         out = jnp.dot(high_part, y, preferred_element_type=F32)
         out = out + jnp.dot(middle, y, preferred_element_type=F32)
         return out + jnp.dot(low_part, y, preferred_element_type=F32)
-
-    def product(k, f):
-        return lambda n: [k[n, t] * f[n, t] for t in range(4)]
-
-    def product1(k, f):
-        return lambda n, t: k[n, t] * f[n, t]
 
     def band_speed(c):
         for copy in k_loads[c]:
@@ -457,66 +469,55 @@
         for copy, there, _ in p_copies[c]:
             start_all([copy], there)
 
-    def coarse_sweep(c, old, new, slots):
-        def sa(q):
-            u = {slot: old[q + 1, slot] for slot in slots}
-            s = []
-            for slot in slots:
-                up, dn = rs(u[slot], 1), rs(u[slot], -1)
-                if slot - 1 in u:
-                    up = jnp.where(m0, rs(u[slot - 1], -3), up)
-                if slot + 1 in u:
-                    dn = jnp.where(m3, rs(u[slot + 1], 3), dn)
-                s.append(up + dn)
-            return s, [u[slot] + 0.5 * x for slot, x in zip(slots, s)]
-
-        def finalize(q, i, near):
-            for n, slot in enumerate(slots):
-                new[q + 1, slot] = 0.2 * old[q + 1, slot] + PC[c, slot, q] + QC[c, slot, q] * near[n]
-
-        along(0, 8, sa, finalize, begin(sa, 0))
-        coarse_pads(new, slots)
-
-    def coarse_pads(ref, slots):
+    def coarse_sweep(c, u, slots):
+        new = {}
         for slot in slots:
-            ref[0, slot] = jnp.where(low_half, 0.0, rs(ref[8, slot], 4))
-            ref[9, slot] = jnp.where(low_half, rs(ref[1, slot], 4), 0.0)
-
-    wide = range(5)
-    narrow = range(1, 4)
+            sums, right, left = [], [], []
+            for q in range(8):
+                above, below = rs(u[slot][q], 1), rs(u[slot][q], -1)
+                if slot > 0:
+                    above = jnp.where(m0, rs(u[slot - 1][q], -3), above)
+                if slot < 4:
+                    below = jnp.where(m3, rs(u[slot + 1][q], 3), below)
+                s = above + below
+                a = u[slot][q] + 0.5 * s
+                sums.append(s)
+                right.append(rl(a, 1))
+                left.append(rl(a, -1))
+            right_pad = jnp.where(low_half, 0.0, rs(right[7], 4))
+            left_pad = jnp.where(low_half, rs(left[0], 4), 0.0)
+            new[slot] = [
+                0.2 * u[slot][q] + PC[c, slot, q] + QC[c, slot, q] * (
+                    sums[q]
+                    + jnp.where(lane0, right[q - 1] if q else right_pad, right[q])
+                    + jnp.where(lane127, left[q + 1] if q < 7 else left_pad, left[q])
+                )
+                for q in range(8)
+            ]
+        return {**u, **new}
 
     def up(c):
         kl, cl_, wl, fl, gl = View(KL, c), View(CL, c), View(WL, c), View(FL, c), View(GL, c)
         kh, ch, wh, fh, gh = View(KH, c), View(CH, c), View(WH, c), View(FH, c), View(GH, c)
-        uc, uq, rsum, rhal = View(UC, c), View(UP, c), View(RS, c), View(RH, c)
+        rsum, rhal = View(RS, c), View(RH, c)
         for copy, _, back in q_copies[c] + p_copies[c]:
             recv_all([copy], back)
-        for slot in range(5):
-            uc[pl.ds(1, 8), slot] = PC[c, slot]
-        coarse_pads(uc, wide)
-
-        def two_sweeps(n, _):
-            coarse_sweep(c, uc, uq, wide)
-            coarse_sweep(c, uq, uc, wide)
-            return 0
-
-        lax.fori_loop(0, 2, two_sweeps, 0)
-        coarse_sweep(c, uc, uq, narrow)
-        coarse_sweep(c, uq, uc, narrow)
-        coarse_sweep(c, uc, uq, narrow)
-
-        own = uq[pl.ds(1, 8), 2] * ICK[c, pl.ds(0, 8)]
+        u = {slot: [PC[c, slot, q] for q in range(8)] for slot in range(5)}
+        for slots in (range(5),) * 4 + (range(1, 4),) * 3:
+            u = coarse_sweep(c, u, slots)
+
+        own = jnp.concatenate([u[2][q] * ICK[c, q] for q in range(8)], axis=0)
         beside = []
         for q in range(4):
-            above0, below0 = uq[q + 1, 1], uq[q + 1, 3]
-            above1, below1 = uq[q + 5, 1], uq[q + 5, 3]
+            above0, below0 = u[1][q], u[3][q]
+            above1, below1 = u[1][q + 4], u[3][q + 4]
             rows = jnp.where(
                 quarter_even,
                 jnp.where(side0, rs(above0, -3), rs(below0, 1)),
                 jnp.where(side0, rs(above1, -1), rs(below1, 3)),
             )
             beside.append(rows * ICK[c, 8 + q])
-        rsum[...] = exact_dot(own.reshape(64, 128), stretch)
+        rsum[...] = exact_dot(own, stretch)
         rhal[...] = exact_dot(jnp.concatenate(beside, axis=0), stretch)
 
         def add_up(count, field, part):
@@ -546,21 +547,6 @@
         halo_stage(product(kh, fh), product1(kl, fl), halo_d)
         pad_local(gl)
         pad_halo(gh, (0, 3))
-
-    def last(c, mass):
-        kl, cl_, wl, gl = View(KL, c), View(CL, c), View(WL, c), View(GL, c)
-        kh, gh, sn, oh, of = View(KH, c), View(GH, c), View(SN, c), View(OH, c), View(OF, c)
-        cells = float(2 * 16 * 8192) * ntiles * ncls
-        ratio = jnp.full((8, 128), target_ref[c] * cells, F32) / mass
-
-        def fine_e(j, i, near):
-            level = ratio * land_local(j)
-            for t in range(4):
-                f = 0.2 * gl[j + 1, t] + cl_[j + 1, t] + wl[j, t] * near[t]
-                oh[j, pl.ds(t, 8, stride=4), :] = f
-                of[j, pl.ds(t, 8, stride=4), :] = tile_of(sn, j, t) * level / jnp.maximum(f, FLOOR_LEVEL)
-
-        local_stage(product(kl, gl), product1(kh, gh), fine_e)
 
     band_speed(0)
     band_speed(1)
@@ -573,8 +559,11 @@
     up(0)
     up(1)
     mass = jnp.full((8, 128), jnp.sum(mass_total(2)), F32)
-    last(0, mass)
-    last(1, mass)
+    cells = float(2 * 16 * 8192) * ntiles * ncls
+    for c in range(2):
+        ratio = jnp.full((8, 128), target_ref[c] * cells, F32) / mass
+        for j in range(32):
+            LV[c, j] = ratio * land_local(j)
 
     for c in range(2):
         sent_all(k_halo[c][0] + b_halo[c][0], has_next)
@@ -586,22 +575,42 @@
             mass_copy(stage, r).wait_send()
 
 
-def write_out(heat, flow, heat_out, flow_out, sem):
+def finish(KL, CL, WL, GL, KH, GH, SN, LV, heat_out, flow_out, OH, OF, sem):
+    *_, local_stage, _, _, _, tile_of, product, product1 = stencil()
     copies = [
-        pltpu.make_async_copy(
-            x.at[c, :, pl.ds(16 * half + 8 * rt, 8), :],
-            out.at[c, rt, pl.ds(32 * half, 32)],
-            sem.at[8 * n + 4 * c + 2 * half + rt],
-        )
-        for n, (x, out) in enumerate(((heat, heat_out), (flow, flow_out)))
+        [
+            pltpu.make_async_copy(
+                x.at[c, :, pl.ds(16 * half + 8 * rt, 8), :],
+                out.at[c, rt, pl.ds(32 * half, 32)],
+                sem.at[8 * n + 4 * c + 2 * half + rt],
+            )
+            for n, (x, out) in enumerate(((OH, heat_out), (OF, flow_out)))
+            for half in range(2)
+            for rt in range(2)
+        ]
         for c in range(2)
-        for half in range(2)
-        for rt in range(2)
     ]
-    for copy in copies:
-        copy.start()
-    for copy in copies:
-        copy.wait()
+
+    def last(c):
+        kl, cl_, wl, gl = View(KL, c), View(CL, c), View(WL, c), View(GL, c)
+        kh, gh, sn, oh, of = View(KH, c), View(GH, c), View(SN, c), View(OH, c), View(OF, c)
+
+        def fine_e(j, i, near):
+            level = LV[c, j]
+            for t in range(4):
+                f = 0.2 * gl[j + 1, t] + cl_[j + 1, t] + wl[j, t] * near[t]
+                oh[j, pl.ds(t, 8, stride=4), :] = f
+                of[j, pl.ds(t, 8, stride=4), :] = tile_of(sn, j, t) * level / jnp.maximum(f, FLOOR_LEVEL)
+
+        local_stage(product(kl, gl), product1(kh, gh), fine_e)
+
+    for c in range(2):
+        last(c)
+        for copy in copies[c]:
+            copy.start()
+    for c in range(2):
+        for copy in copies[c]:
+            copy.wait()
 
 
 def solution(mesh):
@@ -622,23 +631,22 @@
 
         dma = pltpu.SemaphoreType.DMA
         any_space = pl.BlockSpec(memory_space=pl.ANY)
-        heat, flow = pl.pallas_call(
+        parts = pl.pallas_call(
             body,
-            out_shape=[pltpu.VMEM((2, 32, 32, 128), F32)] * 2,
+            out_shape=[
+                vmem(2, 34, 4, 8, 128), vmem(2, 34, 4, 8, 128), vmem(2, 32, 4, 8, 128), vmem(2, 34, 4, 8, 128),
+                vmem(2, 18, 4, 8, 128), vmem(2, 18, 4, 8, 128), vmem(2, 32, 32, 128), vmem(2, 32, 8, 128),
+            ],
             in_specs=[any_space] * 5,
-            out_specs=[pl.BlockSpec(memory_space=pltpu.VMEM)] * 2,
+            out_specs=[pl.BlockSpec(memory_space=pltpu.VMEM)] * 8,
             scratch_shapes=[
-                vmem(2, 32, 32, 128), vmem(2, 32, 32, 128), vmem(2, 32, 32, 128),
+                vmem(2, 32, 32, 128), vmem(2, 32, 32, 128),
                 vmem(2, 16, 32, 128), vmem(2, 16, 32, 128),
-                vmem(2, 34, 4, 8, 128), vmem(2, 34, 4, 8, 128),
-                vmem(2, 32, 4, 8, 128), vmem(2, 32, 4, 8, 128),
-                vmem(2, 34, 4, 8, 128), vmem(2, 34, 4, 8, 128),
-                vmem(2, 18, 4, 8, 128), vmem(2, 18, 4, 8, 128), vmem(2, 16, 4, 8, 128),
-                vmem(2, 18, 4, 8, 128), vmem(2, 18, 4, 8, 128),
+                vmem(2, 32, 4, 8, 128), vmem(2, 34, 4, 8, 128),
+                vmem(2, 18, 4, 8, 128), vmem(2, 16, 4, 8, 128), vmem(2, 18, 4, 8, 128),
                 vmem(2, 64, 512), vmem(2, 32, 512),
                 vmem(2, 8, 8, 128), vmem(2, 8, 8, 128), vmem(2, 12, 8, 128),
                 vmem(2, 5, 8, 8, 128), vmem(2, 5, 8, 8, 128),
-                vmem(2, 10, 5, 8, 128), vmem(2, 10, 5, 8, 128),
                 vmem(3, 8, 128), vmem(20, 8, 128),
                 pltpu.SMEM((8, 32), jnp.int32), pltpu.SMEM((2,), F32),
                 dma((26,)),
@@ -654,13 +662,13 @@
             for x in (tile_mask, target, tiles_view(scaling), tiles_view(source), tiles_view(speed))
         ))
         heat, flow = pl.pallas_call(
-            write_out,
+            finish,
             out_shape=[jax.ShapeDtypeStruct((2, 2, 64, 8, 128), F32)] * 2,
-            in_specs=[any_space] * 2,
+            in_specs=[pl.BlockSpec(memory_space=pltpu.VMEM)] * 8,
             out_specs=[any_space] * 2,
-            scratch_shapes=[dma((16,))],
-            compiler_params=pltpu.CompilerParams(vmem_limit_bytes=4 * 2**20),
-        )(heat, flow)
+            scratch_shapes=[vmem(2, 32, 32, 128), vmem(2, 32, 32, 128), dma((16,))],
+            compiler_params=pltpu.CompilerParams(vmem_limit_bytes=16 * 2**20),
+        )(*parts)
         return rows_view(heat), rows_view(flow)
 
     placed = (P("cls", "tiles", None), P("cls", "tiles", None), P("cls", "tiles", None), P(), P("cls"))

time: 32.2 us -> 31.9 us (level)
  Pallas kernels: 31.3 us -> 30.9 us
    pallas_call x2, Pallas kernels: 31.3 us -> 30.9 us  [the longest x1 29.1 us: on_device(): pl.pallas_call(body, out_shape=[vmem(2, 34, 4, 8, 128), vmem(2, 34, 4, 8,...]
where the time goes in v5:
time: 31.9 us; the launch traced here: 31.6 us
  Pallas kernels  30.9 us (97%)
  between operations  0.64 us (2%)
    pallas_call x1, Pallas kernels, on_device(): pl.pallas_call(body, out_shape=[vmem(2, 34, 4, 8, 128), vmem(2, 34, 4, 8,...  29.1 us
    pallas_call x1, Pallas kernels, on_device(): pl.pallas_call(finish, out_shape=[jax.ShapeDtypeStruct((2, 2, 64, 8, 128)...  1.82 us

profile of v5, /device:TPU:33, one launch (start us, length us, event | category | flops | bytes accessed | tf_op | source)
XLA Modules:
  0.0 31.6 jit_solution(7090669636864519795)
XLA Ops:
  0.6 29.1 %shard_map.68 = (f32[2,34,4,8,128]{4,3,2,1,0:T(8,128)S(1)}, f32[2,34,4,8,128]{4,3,2,1,0:T(8,128)S(1)}, f32[2,32,4,8,128]{4,3,2,1,0:T(8,128)S(1)}, f32[2,34,4,8,1...) custom-call(s32[8,32]{1,0:T(8,128)} %refs_0_.1, ...), custom_call_target="tpu_custom_call" | custom-call | tf_op jit(solution)/shard_map/pallas_call | solution.py:634
  29.8 1.8 %shard_map.69 = (f32[2,2,64,8,128]{4,3,2,1,0:T(8,128)}, f32[2,2,64,8,128]{4,3,2,1,0:T(8,128)}) custom-call(f32[2,34,4,8,128]{4,3,2,1,0:T(8,128)S(1)} %get-tuple-element.12.KL, f32[2,34,4,8,128]{4,3,2,1,0:T(8,128)S(1)} %get-tuple-element.13.CL, f32[2,32,4,8,128]{4,3,2,1,0:T(8,128)S(1)} %get-tuple-element.14.WL, ...), custom_call_target="tpu_custom_call" | custom-call | tf_op jit(solution)/shard_map/pallas_call | solution.py:664

commit v6 on v5

--- a/solution.py
+++ b/solution.py
@@ -200,18 +200,18 @@
         greeted = greeted + jnp.where(there, one, nil)
     pl.semaphore_wait(barrier, greeted)
 
-    def halo_copies(hbm, vmem, c, send, recv):
+    def halo_copies(hbm, vmem, c, send, recv, rows):
         to_next, to_prev = [], []
         for q in range(4):
             n = 8 * c + q
             to_next.append(pltpu.make_async_remote_copy(
-                src_ref=hbm.at[c, 1, pl.ds(16 * q, 16), pl.ds(4, 4), :],
-                dst_ref=vmem.at[c, :, pl.ds(8 * q, 4), :],
+                src_ref=hbm.at[c, 1, pl.ds(16 * q, 16), pl.ds(8 - rows, rows), :],
+                dst_ref=vmem.at[c, :, pl.ds(8 * q + 4 - rows, rows), :],
                 send_sem=send.at[n], recv_sem=recv.at[n],
                 device_id={"tiles": me + 1}, device_id_type=MESH))
             to_prev.append(pltpu.make_async_remote_copy(
-                src_ref=hbm.at[c, 0, pl.ds(16 * q, 16), pl.ds(0, 4), :],
-                dst_ref=vmem.at[c, :, pl.ds(8 * q + 4, 4), :],
+                src_ref=hbm.at[c, 0, pl.ds(16 * q, 16), pl.ds(0, rows), :],
+                dst_ref=vmem.at[c, :, pl.ds(8 * q + 4, rows), :],
                 send_sem=send.at[4 + n], recv_sem=recv.at[4 + n],
                 device_id={"tiles": me - 1}, device_id_type=MESH))
         return to_next, to_prev
@@ -234,12 +234,17 @@
             for copy in copies:
                 copy.wait_send()
 
-    k_halo = [halo_copies(k_in, KHN, c, k_send, k_recv) for c in range(2)]
-    b_halo = [halo_copies(b_in, BHN, c, b_send, b_recv) for c in range(2)]
+    k_halo = [halo_copies(k_in, KHN, c, k_send, k_recv, 4) for c in range(2)]
+    b_halo = [halo_copies(b_in, BHN, c, b_send, b_recv, 3) for c in range(2)]
     for c in range(2):
         for to_next, to_prev in (k_halo[c], b_halo[c]):
             start_all(to_next, has_next)
             start_all(to_prev, has_prev)
+
+    for c in range(2):
+        for q in range(4):
+            for row in (8 * q, 8 * q + 7):
+                BHN[c, :, pl.ds(row, 1), :] = jnp.zeros((16, 1, 128), F32)
 
     def outside(first, there):
         @pl.when(jnp.logical_not(there))

time: 31.9 us -> 31.2 us (0.978)
  Pallas kernels: 30.9 us -> 30.4 us
    pallas_call x1, Pallas kernels: 29.1 us -> 28.6 us  [on_device(): pl.pallas_call(body, out_shape=[vmem(2, 34, 4, 8, 128), vmem(2, 34, 4, 8,...]
where the time goes in v6:
time: 31.2 us; the launch traced here: 31 us
  Pallas kernels  30.4 us (97%)
  between operations  0.64 us (2%)
    pallas_call x1, Pallas kernels, on_device(): pl.pallas_call(body, out_shape=[vmem(2, 34, 4, 8, 128), vmem(2, 34, 4, 8,...  28.6 us
    pallas_call x1, Pallas kernels, on_device(): pl.pallas_call(finish, out_shape=[jax.ShapeDtypeStruct((2, 2, 64, 8, 128)...  1.82 us

profile of v6, /device:TPU:33, one launch (start us, length us, event | category | flops | bytes accessed | tf_op | source)
XLA Modules:
  0.0 31.0 jit_solution(1819601601480802685)
XLA Ops:
  0.6 28.6 %shard_map.68 = (f32[2,34,4,8,128]{4,3,2,1,0:T(8,128)S(1)}, f32[2,34,4,8,128]{4,3,2,1,0:T(8,128)S(1)}, f32[2,32,4,8,128]{4,3,2,1,0:T(8,128)S(1)}, f32[2,34,4,8,1...) custom-call(s32[8,32]{1,0:T(8,128)} %refs_0_.1, ...), custom_call_target="tpu_custom_call" | custom-call | tf_op jit(solution)/shard_map/pallas_call | solution.py:639
  29.2 1.8 %shard_map.69 = (f32[2,2,64,8,128]{4,3,2,1,0:T(8,128)}, f32[2,2,64,8,128]{4,3,2,1,0:T(8,128)}) custom-call(f32[2,34,4,8,128]{4,3,2,1,0:T(8,128)S(1)} %get-tuple-element.12.KL, f32[2,34,4,8,128]{4,3,2,1,0:T(8,128)S(1)} %get-tuple-element.13.CL, f32[2,32,4,8,128]{4,3,2,1,0:T(8,128)S(1)} %get-tuple-element.14.WL, ...), custom_call_target="tpu_custom_call" | custom-call | tf_op jit(solution)/shard_map/pallas_call | solution.py:669
